TPU v7x, 512 devices: a whole 4x8x8 slice. The times are simulated.
512 devices in a mesh: seq: 64 (over y, x, z_hi), tp: 8 (over z_lo, core).
Axes of the slice: x: 4, y: 8, z: 8 (z_hi: 2, z_lo: 4; z = z_hi * 4 + z_lo), core: 2. Of those that a mesh axis runs over, the one named last changes fastest.
Arguments:
- hidden_in: bfloat16 [16384, 2048], P('seq', 'tp'), may hold values from -6 to 6
- w_query: bfloat16 [2048, 2048], P(None, 'tp'), may hold values from -0.375 to 0.375
- w_keyval: bfloat16 [2048, 2, 2048], P(None, None, 'tp'), may hold values from -0.125 to 0.125
- w_out: bfloat16 [2048, 2048], P('tp'), may hold values from -0.125 to 0.125
- prompt_cache: bfloat16 [8192, 2, 2048], P('seq', None, 'tp'), may hold values from -160 to 160
- tail_cache: bfloat16 [128, 128, 2, 2048], P('seq', None, None, 'tp'), may hold values from -6 to 6
- tail_table: int32 [8, 16], replicated, may hold values from 0 to 127, as said below
- tail_len: int32 [8], replicated, may hold values from 1 to 2048
- shared_len: int32 [1], replicated, may hold values from 4096 to 8192
Outputs:
- hidden_out: bfloat16 [16384, 2048], P('seq', 'tp')
- new_cache: bfloat16 [16384, 2, 2048], P('seq', None, 'tp')
Inputs may be any that keep to these rules, and one draw needn't show every extreme that they name: Row r lists each of the slots r * 16 to (r + 1) * 16 - 1 once; block j of request r's tail is held in slot tail_table[r, j].
All inputs are finite; a program needn't handle non-finite values.
Results may differ from a plain program's by a relative error of at most 0.013.
Values may be sent and summed in bfloat16 or wider, within the bound.
A program may use at most 128 MiB of HBM per device.

v0:
```python
import jax
import jax.numpy as jnp
from jax import lax
from jax.sharding import PartitionSpec as P

HD = 128
REQ = 8


NEGATIVE = -1e30


def swapped(value, axis, stride):
    mask = 2**stride
    pairs = [(source, source ^ mask) for source in range(lax.axis_size(axis))]
    return lax.ppermute(value, axis, pairs)


def layer_norm(inputs):
    values = inputs.astype(jnp.float32)
    mean = jnp.mean(values, axis=-1, keepdims=True)
    centred = values - mean
    spread = jnp.mean(centred * centred, axis=-1, keepdims=True)
    return (centred * lax.rsqrt(spread + 1e-05)).astype(jnp.bfloat16)


def rotate(vectors, positions):
    half = vectors.shape[-1] // 2
    freqs = 10000.0 ** (-jnp.arange(half, dtype=jnp.float32) / half)
    angles = positions.astype(jnp.float32)[:, None, None] * freqs
    cosine = jnp.cos(angles)
    sine = jnp.sin(angles)
    first = vectors[..., :half]
    second = vectors[..., half:]
    return jnp.concatenate(
        [first * cosine - second * sine, second * cosine + first * sine], axis=-1
    )


def start_state(heads, queries, width):
    return (
        jnp.full((heads, queries), NEGATIVE, jnp.float32),
        jnp.zeros((heads, queries), jnp.float32),
        jnp.zeros((heads, queries, width), jnp.float32),
    )


def absorb(state, queries, keys, values, allowed):
    scores = jnp.einsum("hqd,khd->hqk", queries, keys, preferred_element_type=jnp.float32) * HD ** (
        -0.5
    )
    scores = jnp.where(allowed[None], scores, -jnp.inf)
    old_top, old_total, old_mixed = state
    new_top = jnp.maximum(old_top, jnp.max(scores, axis=2))
    factor = jnp.exp(old_top - new_top)
    weights = jnp.exp(scores - new_top[:, :, None])
    total = old_total * factor + jnp.sum(weights, axis=2)
    mixed = old_mixed * factor[:, :, None] + jnp.einsum(
        "hqk,khd->hqd", weights.astype(jnp.bfloat16), values, preferred_element_type=jnp.float32
    )
    return (new_top, total, mixed)


def combine(first, second):
    top = jnp.maximum(first[0], second[0])
    left = jnp.exp(first[0] - top)
    right = jnp.exp(second[0] - top)
    return (
        top,
        first[1] * left + second[1] * right,
        first[2] * left[:, :, None] + second[2] * right[:, :, None],
    )


def block_numbers(table_row, slot_ids):
    matches = table_row[None, :] == slot_ids[:, None]
    return jnp.sum(
        jnp.where(matches, jnp.arange(table_row.shape[0], dtype=jnp.int32)[None, :], 0), axis=1
    )


def local(
    hidden_in, w_query, w_keyval, w_out, prompt_cache, tail_cache, tail_table, tail_len, shared_len
):
    local_rows = hidden_in.shape[0]
    heads_here = w_query.shape[1] // HD
    group = lax.axis_size("seq") // REQ
    levels = group.bit_length() - 1
    seq_index = lax.axis_index("seq")
    request = seq_index // group
    member = seq_index % group
    offset = member * local_rows
    prompt_length = shared_len[0]
    own_length = lax.dynamic_index_in_dim(tail_len, request, 0, keepdims=False)
    table_row = lax.dynamic_index_in_dim(tail_table, request, 0, keepdims=False)
    slot_rows = tail_cache.shape[0]
    block_size = tail_cache.shape[1]
    whole = lax.all_gather(hidden_in, "tp", axis=1, tiled=True)
    normed = layer_norm(whole)
    query = jnp.dot(normed, w_query, preferred_element_type=jnp.float32).reshape(
        local_rows, heads_here, HD
    )
    projected = jnp.dot(
        normed, w_keyval.reshape(w_keyval.shape[0], -1), preferred_element_type=jnp.float32
    )
    projected = projected.reshape(local_rows, 2, heads_here, HD)
    positions = prompt_length + own_length + offset + jnp.arange(local_rows, dtype=jnp.int32)
    query = rotate(query, positions).astype(jnp.bfloat16)
    new_keys = rotate(projected[:, 0], positions).astype(jnp.bfloat16)
    new_values = projected[:, 1].astype(jnp.bfloat16)
    new_cache = jnp.stack(
        [new_keys.reshape(local_rows, -1), new_values.reshape(local_rows, -1)], axis=1
    )
    head_query = query.transpose(1, 0, 2)
    piece = lax.all_gather(prompt_cache, "seq", axis=0, tiled=True)
    length = piece.shape[0]
    allowed = (jnp.arange(length, dtype=jnp.int32) < prompt_length)[None, :]
    split = piece.reshape(length, 2, heads_here, HD)
    prompt_state = absorb(
        start_state(heads_here, local_rows, HD), head_query, split[:, 0], split[:, 1], allowed
    )
    packed = jnp.concatenate(
        [tail_cache.reshape(slot_rows * block_size, 2, tail_cache.shape[3]), new_cache], axis=0
    )
    per_member = packed.shape[0]
    for level in range(levels):
        other = swapped(packed, "seq", level)
        upper_half = seq_index // 2**level % 2 == 1
        packed = jnp.where(
            upper_half,
            jnp.concatenate([other, packed], axis=0),
            jnp.concatenate([packed, other], axis=0),
        )
    packed = packed.reshape(group, per_member, 2, heads_here, HD)
    tail_part = packed[:, : slot_rows * block_size].reshape(
        group * slot_rows * block_size, 2, heads_here, HD
    )
    fresh_part = packed[:, slot_rows * block_size :].reshape(group * local_rows, 2, heads_here, HD)
    slot_ids = request * group * slot_rows + jnp.arange(group * slot_rows, dtype=jnp.int32)
    tail_positions = (
        block_numbers(table_row, slot_ids)[:, None] * block_size
        + jnp.arange(block_size, dtype=jnp.int32)[None, :]
    ).reshape(-1)
    tail_allowed = (tail_positions < own_length)[None, :]
    fresh_allowed = (
        jnp.arange(group * local_rows, dtype=jnp.int32)[None, :]
        <= offset + jnp.arange(local_rows, dtype=jnp.int32)[:, None]
    )
    group_state = absorb(
        start_state(heads_here, local_rows, HD),
        head_query,
        tail_part[:, 0],
        tail_part[:, 1],
        tail_allowed,
    )
    group_state = absorb(group_state, head_query, fresh_part[:, 0], fresh_part[:, 1], fresh_allowed)
    final = combine(prompt_state, group_state)
    attended = (
        (final[2] / final[1][:, :, None])
        .astype(jnp.bfloat16)
        .transpose(1, 0, 2)
        .reshape(local_rows, -1)
    )
    summed = lax.psum_scatter(
        lax.dot_general(
            w_out, attended, (((0,), (1,)), ((), ())), preferred_element_type=jnp.float32
        ).astype(jnp.bfloat16),
        "tp",
        scatter_dimension=0,
        tiled=True,
    ).astype(jnp.float32)
    hidden_out = (hidden_in.astype(jnp.float32) + summed.T).astype(jnp.bfloat16)
    return (hidden_out, new_cache)


def solution(mesh):
    return jax.shard_map(
        local,
        mesh=mesh,
        in_specs=(
            P("seq", "tp"),
            P(None, "tp"),
            P(None, None, "tp"),
            P("tp", None),
            P("seq", None, "tp"),
            P("seq", None, None, "tp"),
            P(),
            P(),
            P(),
        ),
        out_specs=(P("seq", "tp"), P("seq", None, "tp")),
        check_vma=False,
    )
```

profile of v0, /device:TPU:1, one launch (start us, length us, event | category | flops | bytes accessed | tf_op | source)
XLA Modules:
  0.0 376.4 jit_solution(9868190781230296545)
XLA Ops:
  7.2 0.0 copy-start
  7.2 0.0 all-gather.3.cloned.1.call-start
  7.2 0.7 all-gather.3.cloned.1.call-update
  7.9 0.0 all-gather.5.cloned.1.call-start
  8.0 1.7 copy.36
  9.6 0.0 all-gather.5.cloned.1.call-update
  9.7 0.0 reduce-scatter.2.cloned.1.call-start
  10.4 1.1 copy.50
  11.5 0.0 copy-start.17
  11.5 2.0 copy.57
  13.5 2.4 copy.39
  16.0 0.7 dynamic_slice.8
  17.4 0.5 multiply_cosine_fusion
  17.9 33.8 %all-gather.3.cloned.1.call-done = bf16[256,2048]{1,0:T(8,128)(2,1)} async-done(((bf16[256,256]{1,0:T(8,128)(2,1)}), bf16[256,2048]{1,0:T(8,128)(2,1)}) %all-gather.3.cloned.1.call-update) | async-done | bytes 1048592 | tf_op jit(solution)/shard_map/all_gather | solution.py:98
  51.7 1.6 convert_reduce_fusion
  53.3 1.6 fusion.16
  55.0 2.7 fusion.62
  57.8 0.7 fusion.85
  58.5 0.1 copy.52
  58.7 0.1 copy.51
  58.8 0.1 copy.54
  58.9 0.9 subtract_convert_fusion.1
  59.8 0.1 pad_maximum_fusion.1
  59.9 0.1 copy.41
  60.1 5.1 %collective-permute-start = (bf16[512,2,256]{0,2,1:T(8,128)(2,1)S(1)}, bf16[512,2,256]{0,2,1:T(8,128)(2,1)S(1)}, u32[]{:S(2)}, u32[]{:S(2)}) collective-permute-start(bf16[512,2,256]{0,2,1:T(8,128)(2,1)S(1)} %maximum_maximum_fusion), channel_id=1, source_target_pairs={{0,8},{8,0},{16,24},{24,16},{32,40},{40,32},{48,56},{56,48},{64,72... | collective-permute-start | bytes 1572872 | tf_op jit(solution)/shard_map/ppermute | solution.py:16
  65.2 25.1 %collective-permute-done = bf16[512,2,256]{0,2,1:T(8,128)(2,1)S(1)} collective-permute-done((bf16[512,2,256]{0,2,1:T(8,128)(2,1)S(1)}, bf16[512,2,256]{0,2,1:T(8,128)(2,1)S(1)}, u32[]{:S(2)}, u32[]{:S(2)}) %collective-permute-start) | collective-permute-done | bytes 524320 | tf_op jit(solution)/shard_map/ppermute | solution.py:16
  90.3 0.3 maximum_select_fusion.2
  90.6 3.1 collective-permute-start.1
  93.7 22.4 %collective-permute-done.1 = bf16[1024,2,256]{0,2,1:T(8,128)(2,1)} collective-permute-done((bf16[1024,2,256]{0,2,1:T(8,128)(2,1)S(1)}, bf16[1024,2,256]{0,2,1:T(8,128)(2,1)}, u32[]{:S(2)}, u32[]{:S(2)}) %collective-permute-start.1) | collective-permute-done | bytes 1048608 | tf_op jit(solution)/shard_map/ppermute | solution.py:16
  116.1 3.0 maximum_select_fusion.1
  119.1 4.8 %collective-permute-start.2 = (bf16[2048,2,256]{0,2,1:T(8,128)(2,1)S(1)}, bf16[2048,2,256]{0,2,1:T(8,128)(2,1)}, u32[]{:S(2)}, u32[]{:S(2)}) collective-permute-start(bf16[2048,2,256]{0,2,1:T(8,128)(2,1)S(1)} %maximum_select_fusion.1), channel_id=1, source_target_pairs={{0,32},{8,40},{16,48},{24,56},{32,0},{40,8},{48,16},{56,24},{64,96... | collective-permute-start | bytes 6291464 | tf_op jit(solution)/shard_map/ppermute | solution.py:16
  123.9 0.7 dynamic-slice_bitcast_fusion
  124.6 0.2 select_reduce_fusion
  124.8 0.8 fusion.65
  125.6 1.2 iota_compare_fusion
  126.7 40.9 %collective-permute-done.2 = bf16[2048,2,256]{0,2,1:T(8,128)(2,1)} collective-permute-done((bf16[2048,2,256]{0,2,1:T(8,128)(2,1)S(1)}, bf16[2048,2,256]{0,2,1:T(8,128)(2,1)}, u32[]{:S(2)}, u32[]{:S(2)}) %collective-permute-start.2) | collective-permute-done | bytes 2097184 | tf_op jit(solution)/shard_map/ppermute | solution.py:16
  167.7 3.7 maximum_select_fusion
  171.4 2.2 copy.58
  173.7 1.7 fusion.87
  175.3 4.6 %copy.56 = bf16[8,256,2,2,128]{4,1,0,3,2:T(8,128)(2,1)} copy(bf16[8,256,2,2,128]{1,0,4,3,2:T(8,128)(2,1)} %get-tuple-element.6) | data formatting | bytes 4194304
  179.9 2.9 copy.55
  182.9 2.2 fusion.7
  185.1 1.2 fusion.8
  186.3 0.7 copy-done.1
  187.1 1.3 copy-done.4
  188.3 2.0 fusion.9
  190.3 107.2 %all-gather.5.cloned.1.call-done = bf16[8192,2,256]{0,2,1:T(8,128)(2,1)} async-done(((bf16[128,2,256]{0,2,1:T(8,128)(2,1)}), bf16[8192,2,256]{0,2,1:T(8,128)(2,1)}) %all-gather.5.cloned.1.call-update) | async-done | bytes 8388624 | tf_op jit(solution)/shard_map/all_gather | solution.py:115
  297.5 9.6 %fusion = (f32[2,256]{1,0:T(2,128)S(1)}, f32[2,256,8192]{2,1,0:T(8,128)}) fusion(pred[8192]{0:T(1024)(128)(4,1)S(1)} %iota_compare_fusion.1, bf16[8192,2,2,128]{0,3,2,1:T(8,128)(2,1)} %bitcast.195, bf16[256,2,64]{2,0,1:T(8,128)(2,1)S(1)} %copy-done.14, bf16[256,2,64]{2,0,1:T(8,128)(2,1)S(1)} %copy-done.13), kind=kOutput, calls=%fused_computation.2 | convolution fusion | flops 1086586368 | bytes 21112832 | tf_op jit(solution)/shard_map/hqd,khd->hqk/dot_general | solution.py:49
  307.1 9.9 %fusion.1 = f32[2,256]{1,0:T(2,128)S(1)} fusion(f32[2,256,8192]{2,1,0:T(8,128)} %get-tuple-element.31, f32[2,256]{1,0:T(2,128)S(1)} %broadcast_maximum_fusion.1, pred[8192]{0:T(1024)(128)(4,1)S(1)} %iota_compare_fusion.1), kind=kLoop, calls=%fused_computation.3 | loop fusion | flops 16776704 | bytes 16789504 | tf_op jit(solution)/shard_map/reduce_sum | solution.py:57
  317.1 0.0 copy-start.9
  317.1 0.0 copy-done.2
  317.1 3.5 fusion.51
  320.6 0.0 copy-done.5
  320.7 0.5 copy-done.9
  321.2 1.3 fusion.45
  322.5 2.1 copy-done.10
  324.6 7.8 %fusion.57 = bf16[256,2,128]{0,2,1:T(8,128)(2,1)S(1)} fusion(f32[256,2,128]{0,2,1:T(8,128)S(1)} %fusion.45, bf16[8192,2,2,128]{0,3,2,1:T(8,128)(2,1)S(1)} %bitcast.196, f32[2,256,8192]{2,1,0:T(8,128)} %get-tuple-element.31, f32[2,256]{1,0:T(2,128)S(1)} %broadcast_maximum_fusion.1, pred[8192]{0:T(1024)(128)(4,1)S(1)} %iota_compare_fusion.1, ...), kind=kOutput, calls=%fused_computation.46 | convolution fusion | flops 1090846720 | bytes 21381120 | tf_op jit(solution)/shard_map/hqk,khd->hqd/dot_general | solution.py:58
  332.4 0.0 copy-start.15
  332.4 1.4 fusion.15
  333.9 0.0 reduce-scatter.2.cloned.1.call-update
  333.9 0.0 copy-done.12
  333.9 0.9 copy.46
  334.8 33.5 %reduce-scatter.2.cloned.1.call-done = bf16[256,256]{0,1:T(8,128)(2,1)} async-done(((bf16[2048,256]{0,1:T(8,128)(2,1)}), bf16[256,256]{0,1:T(8,128)(2,1)}) %reduce-scatter.2.cloned.1.call-update) | async-done | bytes 131088 | tf_op jit(solution)/shard_map/reduce_scatter | solution.py:164
  368.3 1.6 fusion.64
  (41 shorter events, 0.3 us)
Async XLA Ops:
  7.2 325.3 %copy-start = (bf16[256,2048]{1,0:T(8,128)(2,1)S(1)}, bf16[256,2048]{1,0:T(8,128)(2,1)}, u32[]{:S(2)}) copy-start(bf16[256,2048]{1,0:T(8,128)(2,1)} %param.12) | copy-start | bytes 3145732
  7.2 44.5 %all-gather.3.cloned.1.call-start = ((), (), s32[]{:S(2)}) async-start(), calls=%async_computation.1 | async-start | bytes 1179648 | tf_op jit(solution)/shard_map/all_gather | solution.py:98
  7.9 289.6 %all-gather.5.cloned.1.call-start = ((), (), s32[]{:S(2)}) async-start(), calls=%async_computation.2 | async-start | bytes 8519680 | tf_op jit(solution)/shard_map/all_gather | solution.py:115
  9.7 358.6 %reduce-scatter.2.cloned.1.call-start = ((), (), s32[]{:S(2)}) async-start(), calls=%async_computation.3 | async-start | bytes 1179648 | tf_op jit(solution)/shard_map/reduce_scatter | solution.py:164
  11.5 4.5 %copy-start.17 = (s32[8]{0:T(128)S(1)}, s32[8]{0:T(128)}, u32[]{:S(2)}) copy-start(s32[8]{0:T(128)} %param.16) | copy-start | bytes 100
  51.7 6.1 %copy-start.6 = (bf16[256,2048]{1,0:T(8,128)(2,1)S(1)}, bf16[256,2048]{1,0:T(8,128)(2,1)}, u32[]{:S(2)}) copy-start(bf16[256,2048]{1,0:T(8,128)(2,1)} %all-gather.3.cloned.1.call-done) | copy-start | bytes 3145732
  51.7 6.1 %copy-start.16 = (bf16[2048,256]{1,0:T(8,128)(2,1)S(1)}, bf16[2048,256]{1,0:T(8,128)(2,1)}, u32[]{:S(2)}) copy-start(bf16[2048,256]{1,0:T(8,128)(2,1)} %param.10) | copy-start | bytes 3145732
  60.1 33.7 %copy-start.11 = (bf16[256,2,128]{0,2,1:T(8,128)(2,1)}, bf16[256,2,128]{0,2,1:T(8,128)(2,1)S(1)}, u32[]{:S(2)}) copy-start(bf16[256,2,128]{0,2,1:T(8,128)(2,1)S(1)} %copy.41) | copy-start | bytes 393220
  60.1 30.2 %collective-permute-start = (bf16[512,2,256]{0,2,1:T(8,128)(2,1)S(1)}, bf16[512,2,256]{0,2,1:T(8,128)(2,1)S(1)}, u32[]{:S(2)}, u32[]{:S(2)}) collective-permute-start(bf16[512,2,256]{0,2,1:T(8,128)(2,1)S(1)} %maximum_maximum_fusion), channel_id=1, source_target_pairs={{0,8},{8,0},{16,24},{24,16},{32,40},{40,32},{48,56},{56,48},{64,72... | collective-permute-start | bytes 1572872 | tf_op jit(solution)/shard_map/ppermute | solution.py:16
  90.6 3.1 copy-start.3
  90.6 25.5 %collective-permute-start.1 = (bf16[1024,2,256]{0,2,1:T(8,128)(2,1)S(1)}, bf16[1024,2,256]{0,2,1:T(8,128)(2,1)}, u32[]{:S(2)}, u32[]{:S(2)}) collective-permute-start(bf16[1024,2,256]{0,2,1:T(8,128)(2,1)S(1)} %maximum_select_fusion.2), channel_id=1, source_target_pairs={{0,16},{8,24},{16,0},{24,8},{32,48},{40,56},{48,32},{56,40},{64,80... | collective-permute-start | bytes 3145736 | tf_op jit(solution)/shard_map/ppermute | solution.py:16
  119.1 48.6 %collective-permute-start.2 = (bf16[2048,2,256]{0,2,1:T(8,128)(2,1)S(1)}, bf16[2048,2,256]{0,2,1:T(8,128)(2,1)}, u32[]{:S(2)}, u32[]{:S(2)}) collective-permute-start(bf16[2048,2,256]{0,2,1:T(8,128)(2,1)S(1)} %maximum_select_fusion.1), channel_id=1, source_target_pairs={{0,32},{8,40},{16,48},{24,56},{32,0},{40,8},{48,16},{56,24},{64,96... | collective-permute-start | bytes 6291464 | tf_op jit(solution)/shard_map/ppermute | solution.py:16
  175.3 7.5 %copy-start.13 = (bf16[256,2,64]{2,0,1:T(8,128)(2,1)S(1)}, bf16[256,2,64]{2,0,1:T(8,128)(2,1)}, u32[]{:S(2)}) copy-start(bf16[256,2,64]{2,0,1:T(8,128)(2,1)} %get-tuple-element.8) | copy-start | bytes 196612
  175.3 7.5 %copy-start.14 = (bf16[256,2,64]{2,0,1:T(8,128)(2,1)S(1)}, bf16[256,2,64]{2,0,1:T(8,128)(2,1)}, u32[]{:S(2)}) copy-start(bf16[256,2,64]{2,0,1:T(8,128)(2,1)} %get-tuple-element.9) | copy-start | bytes 196612
  182.9 2.2 copy-start.7
  182.9 2.2 copy-start.8
  185.1 2.0 copy-start.1
  186.3 2.0 copy-start.4
  307.1 10.0 %copy-start.2 = (bf16[8,256,2,2,128]{4,1,0,3,2:T(8,128)(2,1)S(1)}, bf16[8,256,2,2,128]{4,1,0,3,2:T(8,128)(2,1)}, u32[]{:S(2)}) copy-start(bf16[8,256,2,2,128]{4,1,0,3,2:T(8,128)(2,1)} %copy.55) | copy-start | bytes 6291460
  317.1 3.6 copy-start.5
  317.1 4.1 %copy-start.9 = (bf16[8,256,2,2,128]{4,1,0,3,2:T(8,128)(2,1)S(1)}, bf16[8,256,2,2,128]{4,1,0,3,2:T(8,128)(2,1)}, u32[]{:S(2)}) copy-start(bf16[8,256,2,2,128]{4,1,0,3,2:T(8,128)(2,1)} %copy.56) | copy-start | bytes 6291460
  321.2 3.4 copy-start.10
  324.6 9.3 %copy-start.12 = (bf16[256,2,128]{0,2,1:T(8,128)(2,1)S(1)}, bf16[256,2,128]{0,2,1:T(8,128)(2,1)}, u32[]{:S(2)}) copy-start(bf16[256,2,128]{0,2,1:T(8,128)(2,1)} %copy-done.11) | copy-start | bytes 393220
  332.4 35.9 %copy-start.15 = (bf16[256,256]{1,0:T(8,128)(2,1)S(1)}, bf16[256,256]{1,0:T(8,128)(2,1)}, u32[]{:S(2)}) copy-start(bf16[256,256]{1,0:T(8,128)(2,1)} %param.9) | copy-start | bytes 393220
Sparse Core Ops, SparseCore 0:
  10.0 41.6 all-gather.2
  56.0 241.4 all-gather.4
  334.0 34.2 reduce-scatter.1
where the time goes:
time: 379 us; the launch traced here: 376 us
  waiting for transfers between devices  264 us (70%)
  matrix products  30.5 us (8%)
  other arithmetic  27.6 us (7%)
  local copies, waits for them, and re-layouts  26.1 us (7%)
  between operations  15.6 us (4%)
  starting transfers between devices  13 us (3%)
    all_gather x1, waiting for transfers between devices, local(): piece = lax.all_gather(prompt_cache, 'seq', axis=0, tiled=True)  107 us
    ppermute x3, waiting for transfers between devices, swapped(): return lax.ppermute(value, axis, pairs)  88.4 us
    all_gather x1, waiting for transfers between devices, local(): whole = lax.all_gather(hidden_in, 'tp', axis=1, tiled=True)  33.8 us
    reduce_scatter x1, waiting for transfers between devices, local(): lax.psum_scatter(lax.dot_general(w_out, attended, (((0,), (1,)), ((), ())...  33.5 us
    unnamed x45, local copies, waits for them, and re-layouts  19.4 us
    dot_general x3, matrix products, absorb(): jnp.einsum('hqd,khd->hqk', queries, keys, preferred_element_type=jnp.floa...  13 us
    ppermute x3, starting transfers between devices, swapped(): return lax.ppermute(value, axis, pairs)  12.9 us
    dot_general x3, matrix products, absorb(): jnp.einsum('hqk,khd->hqd', weights.astype(jnp.bfloat16), values, preferre...  12.6 us
  transfers between devices with their start and end apart: 6, of which 6 were waited for; matrix products, arithmetic and copies ran while one was open for 12% of the time, Pallas kernels for 0%

commit v1 on v0

v1 whole, which is shorter than its diff:
```python
import functools

import jax
import jax.numpy as jnp
from jax import lax
from jax.experimental import pallas as pl
from jax.experimental.pallas import tpu as pltpu
from jax.sharding import PartitionSpec as P

HD = 128
REQ = 8
ROWS = 256
COLS = 256
TPN = 8
KEYS = 1536
NEG = -1e30
SCALE = HD**-0.5 * 1.4426950408889634
MESH = pl.DeviceIdType.MESH


def flip(v, d):
    low = (v % 2 + d % 2) % 2
    high = (v // 2 + d // 2) % 2
    return low + 2 * high


def slot_offsets(i):
    e = i // 4
    r = (i - 3 * e) % 4
    d = r + r // 2 - 2 * (r // 3)
    return d, e


def mix(parts, stats):
    top = functools.reduce(jnp.maximum, [s[0:2] for s in stats])
    raw = [s[2:4] * jnp.exp2(s[0:2] - top) for s in stats]
    total = sum(raw)
    weights = [w / total for w in raw]
    pad = jnp.zeros((128 - 2 * len(stats), ROWS), jnp.float32)
    columns = jnp.concatenate(weights + [pad], axis=0).T
    heads = []
    for h in range(2):
        lanes = slice(h * HD, (h + 1) * HD)
        heads.append(
            sum(
                columns[:, 2 * j + h : 2 * j + h + 1] * part[:, lanes].astype(jnp.float32)
                for j, part in enumerate(parts)
            )
        )
    return jnp.concatenate(heads, axis=1), top, total


def kernel(
    shared_ref, tail_len_ref, table_ref, hid, wq_hbm, wkv_hbm, wo_hbm, prompt, tail_hbm, cos_ref,
    sin_ref, out_ref, nc_ref,
    hbuf, wq, wkv, wo, kv, bias, qbuf, obuf, sbuf, obuf_in, sbuf_in, zo, zs, zo_in, zs_in,
    pair_out, pair_in, acc, rs_out, rs_in,
    lsem, p_send, p_recv, h_send, h_recv, g_send, g_recv, q_send, q_recv, o_send, o_recv,
    s_send, s_recv, w_send, w_recv, r_send, r_recv,
):
    s = lax.axis_index("seq")
    t = lax.axis_index("tp")
    y, x, zh = s // 8, (s // 2) % 4, s % 2
    zl, c = t // 2, t % 2
    member = s % 8
    pair = (s, zl * 2 + 1 - c)
    zpeer = (y * 8 + x * 2 + 1 - zh, t)

    def tp_peer(d):
        return (s, flip(zl, d) * 2 + c)

    def x_peer(d):
        return (y * 8 + flip(x, d) * 2 + zh, t)

    def y_peer(d):
        return (((y + d) % 8) * 8 + x * 2 + zh, t)

    def remote(src, dst, send, recv, device):
        return pltpu.make_async_remote_copy(
            src_ref=src, dst_ref=dst, send_sem=send, recv_sem=recv, device_id=device,
            device_id_type=MESH,
        )

    local = [
        pltpu.make_async_copy(wq_hbm, wq, lsem.at[0]),
        pltpu.make_async_copy(wkv_hbm, wkv, lsem.at[1]),
        pltpu.make_async_copy(wo_hbm, wo, lsem.at[2]),
        pltpu.make_async_copy(tail_hbm, kv.at[pl.ds(256, 256), :], lsem.at[3]),
    ]
    for copy in local:
        copy.start()

    barrier = pltpu.get_barrier_semaphore()
    peers = [pair, zpeer]
    peers += [tp_peer(d) for d in (1, 2, 3)]
    peers += [x_peer(d) for d in (1, 2, 3)]
    peers += [y_peer(d) for d in range(1, 8)]
    for peer in peers:
        pl.semaphore_signal(barrier, inc=1, device_id=peer, device_id_type=MESH)
    pl.semaphore_wait(barrier, len(peers))

    h_copies = {}
    for d in (3, 2, 1):
        h_copies[d] = remote(hid, hbuf.at[t], h_send.at[d], h_recv.at[d], tp_peer(d))
        h_copies[d].start()
    h_copies[0] = remote(hid, hbuf.at[t], h_send.at[0], h_recv.at[0], pair)
    h_copies[0].start()
    p_copies = []
    for d in (4, 3, 5, 2, 6, 1, 7):
        copy = remote(
            prompt, kv.at[pl.ds(512 + d * 128, 128), :], p_send.at[d], p_recv.at[d], y_peer(d)
        )
        copy.start()
        p_copies.append(copy)

    hbuf[t] = hid[...]
    kv[pl.ds(512, 128), :] = prompt[...]
    own_tail = tail_len_ref[y]
    shared = shared_ref[0]
    lane = lax.broadcasted_iota(jnp.int32, (8, 128), 1)
    for k in range(2):
        block = jnp.int32(0)
        for j in range(16):
            block += jnp.where(table_ref[y, j] == s * 2 + k, jnp.int32(j), jnp.int32(0))
        bias[:, k * 128 : (k + 1) * 128] = jnp.where(block * 128 + lane < own_tail, 0.0, NEG)
    for d in range(8):
        start = (((y + 8 - d) % 8) * 8 + x * 2 + zh) * 128
        bias[:, 256 + d * 128 : 384 + d * 128] = jnp.where(start + lane < shared, 0.0, NEG)

    g_copies = []
    for d in (1, 2, 3):
        h_copies[d].wait_recv()
        index = flip(zl, d) * 2 + c
        copy = remote(hbuf.at[index], hbuf.at[index], g_send.at[d], g_recv.at[d], pair)
        copy.start()
        g_copies.append(copy)
    h_copies[0].wait_recv()
    for copy in g_copies:
        copy.wait_recv()

    total = functools.reduce(
        jnp.add, [hbuf[j].astype(jnp.float32) for j in range(TPN)]
    )
    mean = jnp.sum(total, axis=1, keepdims=True) * (1.0 / (TPN * COLS))
    square = jnp.zeros((ROWS, COLS), jnp.float32)
    for j in range(TPN):
        centred = hbuf[j].astype(jnp.float32) - mean
        square += centred * centred
    spread = jnp.sum(square, axis=1, keepdims=True) * (1.0 / (TPN * COLS))
    factor = lax.rsqrt(spread + 1e-05)
    local[0].wait()
    local[1].wait()
    query = jnp.zeros((ROWS, COLS), jnp.float32)
    keyval = jnp.zeros((ROWS, 2 * COLS), jnp.float32)
    for j in range(TPN):
        normed = ((hbuf[j].astype(jnp.float32) - mean) * factor).astype(jnp.bfloat16)
        rows = pl.ds(j * COLS, COLS)
        query += jnp.dot(normed, wq[rows, :], preferred_element_type=jnp.float32)
        keyval += jnp.dot(normed, wkv[rows, :], preferred_element_type=jnp.float32)
    cosine, sine = cos_ref[...], sin_ref[...]

    def rotated(vectors):
        return (vectors * cosine + pltpu.roll(vectors, HD // 2, 1) * sine).astype(jnp.bfloat16)

    for h in range(2):
        lanes = slice(h * HD, (h + 1) * HD)
        qbuf[0, :, lanes] = rotated(query[:, lanes])
    q_copies = {7: remote(qbuf.at[0], qbuf.at[7], q_send.at[7], q_recv.at[7], zpeer)}
    q_copies[7].start()
    for i in (1, 2, 3):
        d, _ = slot_offsets(i)
        q_copies[i] = remote(qbuf.at[0], qbuf.at[i], q_send.at[i], q_recv.at[i], x_peer(d))
        q_copies[i].start()
    for i in (4, 5, 6):
        d, _ = slot_offsets(i)
        q_copies[i] = remote(qbuf.at[7], qbuf.at[i], q_send.at[i], q_recv.at[i], x_peer(d))
    for h in range(2):
        lanes = slice(h * HD, (h + 1) * HD)
        new_key = rotated(keyval[:, lanes])
        kv[pl.ds(0, ROWS), lanes] = new_key
        nc_ref[:, lanes] = new_key
    new_value = keyval[:, COLS:].astype(jnp.bfloat16)
    kv[pl.ds(0, ROWS), COLS:] = new_value
    nc_ref[:, COLS:] = new_value
    local[3].wait()
    for copy in p_copies:
        copy.wait_recv()

    def block(i, carry):
        d, e = slot_offsets(i)
        other = flip(x, d) * 2 + (zh + e) % 2

        @pl.when(i == 2)
        def _():
            q_copies[7].wait_recv()
            for k in (4, 5, 6):
                q_copies[k].start()

        @pl.when((i > 0) & (i < 7))
        def _():
            remote(qbuf.at[0], qbuf.at[i], q_send.at[i], q_recv.at[i], x_peer(d)).wait_recv()

        column = lax.broadcasted_iota(jnp.int32, (ROWS, ROWS), 1)
        row = lax.broadcasted_iota(jnp.int32, (ROWS, ROWS), 0)
        causal = column - row <= (other - member) * ROWS
        tops, totals = [], []
        for h in range(2):
            lanes = slice(h * HD, (h + 1) * HD)
            q = qbuf[i, :, lanes]
            scores = lax.dot_general(
                q, kv[:, lanes], (((1,), (1,)), ((), ())), preferred_element_type=jnp.float32
            ) * SCALE
            fresh = jnp.where(causal, scores[:, :ROWS], NEG)
            cached = scores[:, ROWS:] + bias[0:1, :]
            top = jnp.maximum(
                jnp.max(fresh, axis=1, keepdims=True), jnp.max(cached, axis=1, keepdims=True)
            )
            fresh = jnp.exp2(fresh - top)
            cached = jnp.exp2(cached - top)
            total = jnp.sum(fresh, axis=1, keepdims=True) + jnp.sum(cached, axis=1, keepdims=True)
            mixed = jnp.dot(
                fresh.astype(jnp.bfloat16), kv[0:ROWS, COLS + h * HD : COLS + (h + 1) * HD],
                preferred_element_type=jnp.float32,
            ) + jnp.dot(
                cached.astype(jnp.bfloat16), kv[ROWS:KEYS, COLS + h * HD : COLS + (h + 1) * HD],
                preferred_element_type=jnp.float32,
            )
            obuf[i, :, lanes] = (mixed / total).astype(jnp.bfloat16)
            tops.append(top)
            totals.append(total)
        place = lax.broadcasted_iota(jnp.int32, (ROWS, 128), 1)
        packed = jnp.where(
            place == 0,
            tops[0],
            jnp.where(place == 1, tops[1], jnp.where(place == 2, totals[0], totals[1])),
        )
        sbuf[i] = packed.T[0:8]

        @pl.when((i > 0) & (i < 7))
        def _():
            remote(sbuf.at[i], sbuf_in.at[i], s_send.at[i], s_recv.at[i], x_peer(d)).start()
            remote(obuf.at[i], obuf_in.at[i], o_send.at[i], o_recv.at[i], x_peer(d)).start()

        return carry

    lax.fori_loop(0, 8, block, 0)

    def returned(i):
        d, _ = slot_offsets(i)
        return (
            remote(sbuf.at[i], sbuf_in.at[i], s_send.at[i], s_recv.at[i], x_peer(d)),
            remote(obuf.at[i], obuf_in.at[i], o_send.at[i], o_recv.at[i], x_peer(d)),
        )

    def joined(own, others):
        for i in others:
            for copy in returned(i):
                copy.wait_recv()
        return mix(
            [obuf[own]] + [obuf_in[i] for i in others], [sbuf[own]] + [sbuf_in[i] for i in others]
        )

    mixed, top, total = joined(7, (4, 5, 6))
    zo[...] = mixed.astype(jnp.bfloat16)
    zs[...] = jnp.concatenate([top, total, top, total], axis=0)
    z_copies = [
        remote(zs, zs_in, s_send.at[7], s_recv.at[7], zpeer),
        remote(zo, zo_in, o_send.at[7], o_recv.at[7], zpeer),
    ]
    for copy in z_copies:
        copy.start()
    mixed, top, total = joined(0, (1, 2, 3))
    for copy in z_copies:
        copy.wait_recv()
    mixed, _, _ = mix(
        [mixed, zo_in[...]], [jnp.concatenate([top, total], axis=0), zs_in[...]]
    )
    attended = mixed.astype(jnp.bfloat16)

    local[2].wait()

    def share(d, core):
        start = pl.multiple_of((flip(zl, d) * 2 + core) * COLS, COLS)
        return jnp.dot(attended, wo[:, pl.ds(start, COLS)], preferred_element_type=jnp.float32)

    pair_copies = {}
    for d in (3, 2, 1, 0):
        pair_out[d] = share(d, 1 - c).astype(jnp.bfloat16)
        pair_copies[d] = remote(pair_out.at[d], pair_in.at[d], w_send.at[d], w_recv.at[d], pair)
        pair_copies[d].start()
    for d in (3, 2, 1, 0):
        acc[d] = share(d, c)
    r_copies = {}
    for d in (3, 2, 1):
        pair_copies[d].wait_recv()
        rs_out[d] = (acc[d] + pair_in[d].astype(jnp.float32)).astype(jnp.bfloat16)
        r_copies[d] = remote(rs_out.at[d], rs_in.at[d], r_send.at[d], r_recv.at[d], tp_peer(d))
        r_copies[d].start()
    pair_copies[0].wait_recv()
    summed = hid[...].astype(jnp.float32) + acc[0] + pair_in[0].astype(jnp.float32)
    for d in (1, 2, 3):
        r_copies[d].wait_recv()
        summed += rs_in[d].astype(jnp.float32)
    out_ref[...] = summed.astype(jnp.bfloat16)

    for copies in (h_copies, q_copies, pair_copies, r_copies):
        for copy in copies.values():
            copy.wait_send()
    for copy in p_copies + g_copies + z_copies:
        copy.wait_send()
    for i in range(1, 7):
        for copy in returned(i):
            copy.wait_send()


def local(
    hidden_in, w_query, w_keyval, w_out, prompt_cache, tail_cache, tail_table, tail_len, shared_len
):
    s = lax.axis_index("seq")
    half = HD // 2
    positions = (
        shared_len[0]
        + lax.dynamic_index_in_dim(tail_len, s // REQ, 0, keepdims=False)
        + (s % REQ) * ROWS
        + jnp.arange(ROWS, dtype=jnp.int32)
    )
    freqs = 10000.0 ** (-jnp.arange(half, dtype=jnp.float32) / half)
    angles = positions.astype(jnp.float32)[:, None] * freqs
    cosine, sine = jnp.cos(angles), jnp.sin(angles)
    cosine = jnp.concatenate([cosine, cosine], axis=1)
    sine = jnp.concatenate([-sine, sine], axis=1)
    vmem = pl.BlockSpec(memory_space=pltpu.VMEM)
    smem = pl.BlockSpec(memory_space=pltpu.SMEM)
    anywhere = pl.BlockSpec(memory_space=pl.ANY)
    bf16, f32 = jnp.bfloat16, jnp.float32
    dma = pltpu.SemaphoreType.DMA
    block = (ROWS, COLS)
    out, cache = pl.pallas_call(
        kernel,
        out_shape=(
            jax.ShapeDtypeStruct(block, bf16),
            jax.ShapeDtypeStruct((ROWS, 2 * COLS), bf16),
        ),
        in_specs=[smem, smem, smem, vmem, anywhere, anywhere, anywhere, vmem, anywhere, vmem, vmem],
        out_specs=(vmem, vmem),
        scratch_shapes=[
            pltpu.VMEM((TPN,) + block, bf16),
            pltpu.VMEM((TPN * COLS, COLS), bf16),
            pltpu.VMEM((TPN * COLS, 2 * COLS), bf16),
            pltpu.VMEM((COLS, TPN * COLS), bf16),
            pltpu.VMEM((KEYS, 2 * COLS), bf16),
            pltpu.VMEM((8, KEYS - ROWS), f32),
            pltpu.VMEM((8,) + block, bf16),
            pltpu.VMEM((8,) + block, bf16),
            pltpu.VMEM((8, 8, ROWS), f32),
            pltpu.VMEM((8,) + block, bf16),
            pltpu.VMEM((8, 8, ROWS), f32),
            pltpu.VMEM(block, bf16),
            pltpu.VMEM((8, ROWS), f32),
            pltpu.VMEM(block, bf16),
            pltpu.VMEM((8, ROWS), f32),
            pltpu.VMEM((4,) + block, bf16),
            pltpu.VMEM((4,) + block, bf16),
            pltpu.VMEM((4,) + block, f32),
            pltpu.VMEM((4,) + block, bf16),
            pltpu.VMEM((4,) + block, bf16),
            dma((4,)),
            dma((8,)), dma((8,)),
            dma((4,)), dma((4,)),
            dma((4,)), dma((4,)),
            dma((8,)), dma((8,)),
            dma((8,)), dma((8,)),
            dma((8,)), dma((8,)),
            dma((4,)), dma((4,)),
            dma((4,)), dma((4,)),
        ],
        compiler_params=pltpu.CompilerParams(collective_id=0, has_side_effects=True),
    )(
        shared_len,
        tail_len,
        tail_table,
        hidden_in,
        w_query,
        w_keyval.reshape(TPN * COLS, 2 * COLS),
        w_out,
        prompt_cache.reshape(128, 2 * COLS),
        tail_cache.reshape(ROWS, 2 * COLS),
        cosine,
        sine,
    )
    return (out, cache.reshape(ROWS, 2, COLS))


def solution(mesh):
    return jax.shard_map(
        local,
        mesh=mesh,
        in_specs=(
            P("seq", "tp"),
            P(None, "tp"),
            P(None, None, "tp"),
            P("tp", None),
            P("seq", None, "tp"),
            P("seq", None, None, "tp"),
            P(),
            P(),
            P(),
        ),
        out_specs=(P("seq", "tp"), P("seq", None, "tp")),
        check_vma=False,
    )
```

time: 379 us -> 105 us (0.28)
  waiting for transfers between devices: 264 us -> 0 us
  Pallas kernels: 0 us -> 90.6 us
  matrix products: 30.5 us -> 0 us
  other arithmetic: 27.6 us -> 1.4 us
  local copies, waits for them, and re-layouts: 26.1 us -> 11.2 us
  between operations: 15.6 us -> 1.99 us
  starting transfers between devices: 13 us -> 0 us
    all_gather x2 -> x0, waiting for transfers between devices: 141 us -> none  [the longest x1 107 us: local(): piece = lax.all_gather(prompt_cache, 'seq', axis=0, tiled=True)]
    pallas_call x0 -> x1, Pallas kernels: none -> 90.6 us  [local(): pl.pallas_call(kernel, out_shape=(jax.ShapeDtypeStruct(block, bf16), jax....]
    ppermute x3 -> x0, waiting for transfers between devices: 88.4 us -> none  [swapped(): return lax.ppermute(value, axis, pairs)]
    reduce_scatter x1 -> x0, waiting for transfers between devices: 33.5 us -> none  [local(): lax.psum_scatter(lax.dot_general(w_out, attended, (((0,), (1,)), ((), ())...]
    dot_general x9 -> x0, matrix products: 30.5 us -> none  [the longest x3 13 us: absorb(): jnp.einsum('hqd,khd->hqk', queries, keys, preferred_element_type=jnp.floa...]
    reduce_sum x5 -> x0, other arithmetic: 15.4 us -> none  [the longest x2 12 us: absorb(): total = old_total * factor + jnp.sum(weights, axis=2)]
    ppermute x3 -> x0, starting transfers between devices: 12.9 us -> none  [swapped(): return lax.ppermute(value, axis, pairs)]
    unnamed x45 -> x4, local copies, waits for them, and re-layouts: 19.4 us -> 8.2 us
  transfers between devices with their start and end apart: 6 -> 0, of which waited for: 6 -> 0; matrix products, arithmetic and copies ran while one was open for 12% -> 0% of each run, Pallas kernels for 0% -> 0%
where the time goes in v1:
time: 105 us
  Pallas kernels  90.6 us (86%)
  local copies, waits for them, and re-layouts  11.2 us (11%)
  between operations  1.99 us (2%)
  other arithmetic  1.4 us (1%)
    pallas_call x1, Pallas kernels, local(): pl.pallas_call(kernel, out_shape=(jax.ShapeDtypeStruct(block, bf16), jax....  90.6 us
    unnamed x4, local copies, waits for them, and re-layouts  8.2 us

profile of v1, /device:TPU:1, one launch (start us, length us, event | category | flops | bytes accessed | tf_op | source)
XLA Modules:
  0.0 105.1 jit_solution(16409289967055987027)
XLA Ops:
  1.3 1.2 %dynamic_slice.4 = s32[1]{0:T(128)} dynamic-slice(s32[8]{0:T(128)} %tail_len_ref.1, s32[]{:T(128)S(6)} %select_n.16), dynamic_slice_sizes={1} | dynamic-slice | bytes 12 | tf_op jit(solution)/shard_map/jit(dynamic_index_in_dim)/dynamic_slice | solution.py:323
  3.2 1.6 %copy.12 = bf16[16,8,2,256]{3,1,2,0:T(8,128)(2,1)} copy(bf16[16,8,2,256]{3,2,1,0:T(2,128)(2,1)} %bitcast.13) | data formatting | bytes 262144
  4.8 1.7 %copy.13 = bf16[32,8,2,256]{3,1,2,0:T(8,128)(2,1)} copy(bf16[32,8,2,256]{3,2,1,0:T(2,128)(2,1)} %bitcast.12) | data formatting | bytes 524288
  6.5 0.5 fusion
  7.0 0.8 pad_maximum_fusion
  7.9 3.4 %copy.11 = bf16[256,8,2,256]{3,1,2,0:T(8,128)(2,1)} copy(bf16[256,8,2,256]{3,2,1,0:T(2,128)(2,1)} %bitcast.9) | data formatting | bytes 4194304
  11.2 90.6 %shard_map.104 = (bf16[256,256]{1,0:T(8,128)(2,1)}, bf16[256,512]{1,0:T(8,128)(2,1)}) custom-call(s32[1]{0:T(128)S(6)} %copy.15.shared_ref, s32[8]{0:T(128)} %tail_len_ref.1, s32[8,16]{1,0:T(8,128)} %table_ref.1, bf16[256,256]{1,0:T(8,128)(2,1)} %hid.1, bf16[2048,256]{1,0:T(8,128)(2,1)} %wq_hbm.1, bf16[2048,512]{1,0:T(8,128)(2,1)} %bitcast.8, ...), custom_call_target="tpu_custom_call" | custom-call | tf_op jit(solution)/shard_map/pallas_call | solution.py:338
  101.8 1.7 %reshape.31 = bf16[256,2,256]{2,1,0:T(2,128)(2,1)} reshape(bf16[256,512]{1,0:T(8,128)(2,1)} %get-tuple-element.5) | data formatting | bytes 524288 | tf_op jit(solution)/shard_map/reshape | solution.py:391
  103.5 1.6 %copy.16 = bf16[256,256]{1,0:T(8,128)(2,1)} copy(bf16[256,256]{1,0:T(8,128)(2,1)} %get-tuple-element.13) | data formatting | bytes 262144
  (2 shorter events, 0.0 us)

commit v2 on v1

--- a/solution.py
+++ b/solution.py
@@ -2,6 +2,7 @@
 
 import jax
 import jax.numpy as jnp
+import numpy as np
 from jax import lax
 from jax.experimental import pallas as pl
 from jax.experimental.pallas import tpu as pltpu
@@ -51,9 +52,9 @@
 
 
 def kernel(
-    shared_ref, tail_len_ref, table_ref, hid, wq_hbm, wkv_hbm, wo_hbm, prompt, tail_hbm, cos_ref,
-    sin_ref, out_ref, nc_ref,
-    hbuf, wq, wkv, wo, kv, bias, qbuf, obuf, sbuf, obuf_in, sbuf_in, zo, zs, zo_in, zs_in,
+    shared_ref, tail_len_ref, table_ref, hid, wq_hbm, wkv_hbm, wo_hbm, prompt, tail_hbm,
+    freq_ref, out_ref, nc_ref,
+    hbuf, wq, wkv_raw, wkv, wo, tail_raw, kv, bias, qbuf, obuf, sbuf, obuf_in, sbuf_in, zo, zs, zo_in, zs_in,
     pair_out, pair_in, acc, rs_out, rs_in,
     lsem, p_send, p_recv, h_send, h_recv, g_send, g_recv, q_send, q_recv, o_send, o_recv,
     s_send, s_recv, w_send, w_recv, r_send, r_recv,
@@ -83,18 +84,21 @@
 
     local = [
         pltpu.make_async_copy(wq_hbm, wq, lsem.at[0]),
-        pltpu.make_async_copy(wkv_hbm, wkv, lsem.at[1]),
+        pltpu.make_async_copy(wkv_hbm, wkv_raw, lsem.at[1]),
         pltpu.make_async_copy(wo_hbm, wo, lsem.at[2]),
-        pltpu.make_async_copy(tail_hbm, kv.at[pl.ds(256, 256), :], lsem.at[3]),
+        pltpu.make_async_copy(tail_hbm, tail_raw, lsem.at[3]),
     ]
     for copy in local:
         copy.start()
+
+    kv[pl.ds(512, 128), 0:COLS] = prompt[:, 0, :]
+    kv[pl.ds(512, 128), COLS:] = prompt[:, 1, :]
 
     barrier = pltpu.get_barrier_semaphore()
     peers = [pair, zpeer]
     peers += [tp_peer(d) for d in (1, 2, 3)]
     peers += [x_peer(d) for d in (1, 2, 3)]
-    peers += [y_peer(d) for d in range(1, 8)]
+    peers += [y_peer(1), y_peer(7)]
     for peer in peers:
         pl.semaphore_signal(barrier, inc=1, device_id=peer, device_id_type=MESH)
     pl.semaphore_wait(barrier, len(peers))
@@ -105,16 +109,34 @@
         h_copies[d].start()
     h_copies[0] = remote(hid, hbuf.at[t], h_send.at[0], h_recv.at[0], pair)
     h_copies[0].start()
-    p_copies = []
-    for d in (4, 3, 5, 2, 6, 1, 7):
-        copy = remote(
-            prompt, kv.at[pl.ds(512 + d * 128, 128), :], p_send.at[d], p_recv.at[d], y_peer(d)
-        )
-        copy.start()
-        p_copies.append(copy)
+    def ring(step):
+        first = 64 if step == 4 else 128
+        right = remote(
+            kv.at[pl.ds(512 + (step - 1) * 128, first), :],
+            kv.at[pl.ds(512 + step * 128, first), :],
+            p_send.at[step - 1], p_recv.at[step - 1], y_peer(1),
+        )
+        shift = 128 - first
+        left = remote(
+            kv.at[pl.ds(512 + (9 - step) % 8 * 128 + shift, first), :],
+            kv.at[pl.ds(512 + (8 - step) * 128 + shift, first), :],
+            p_send.at[step + 3], p_recv.at[step + 3], y_peer(7),
+        )
+        return [right, left]
+
+    p_steps = [ring(step) for step in (1, 2, 3, 4)]
+
+    def forward(step):
+        if step > 0:
+            for copy in p_steps[step - 1]:
+                copy.wait_recv()
+        if step < 4:
+            for copy in p_steps[step]:
+                copy.start()
+
+    forward(0)
 
     hbuf[t] = hid[...]
-    kv[pl.ds(512, 128), :] = prompt[...]
     own_tail = tail_len_ref[y]
     shared = shared_ref[0]
     lane = lax.broadcasted_iota(jnp.int32, (8, 128), 1)
@@ -127,6 +149,27 @@
         start = (((y + 8 - d) % 8) * 8 + x * 2 + zh) * 128
         bias[:, 256 + d * 128 : 384 + d * 128] = jnp.where(start + lane < shared, 0.0, NEG)
 
+    positions = shared + own_tail + member * ROWS
+    positions = positions + lax.broadcasted_iota(jnp.int32, (ROWS, HD), 0)
+    angles = positions.astype(jnp.float32) * freq_ref[0:1, :]
+    cosine = jnp.cos(angles)
+    sine = jnp.sin(angles) * freq_ref[1:2, :]
+    local[3].wait()
+    kv[pl.ds(256, 256), 0:COLS] = tail_raw[:, 0, :]
+    kv[pl.ds(256, 256), COLS:] = tail_raw[:, 1, :]
+    local[1].wait()
+
+    def unweave(k, carry):
+        rows = pl.ds(pl.multiple_of(k * 256, 256), 256)
+        wkv[rows, 0:COLS] = wkv_raw[rows, 0, :]
+        wkv[rows, COLS:] = wkv_raw[rows, 1, :]
+        return carry
+
+    lax.fori_loop(0, 4, unweave, 0)
+    forward(1)
+    lax.fori_loop(4, 8, unweave, 0)
+    forward(2)
+
     g_copies = []
     for d in (1, 2, 3):
         h_copies[d].wait_recv()
@@ -134,6 +177,7 @@
         copy = remote(hbuf.at[index], hbuf.at[index], g_send.at[d], g_recv.at[d], pair)
         copy.start()
         g_copies.append(copy)
+    forward(3)
     h_copies[0].wait_recv()
     for copy in g_copies:
         copy.wait_recv()
@@ -149,7 +193,6 @@
     spread = jnp.sum(square, axis=1, keepdims=True) * (1.0 / (TPN * COLS))
     factor = lax.rsqrt(spread + 1e-05)
     local[0].wait()
-    local[1].wait()
     query = jnp.zeros((ROWS, COLS), jnp.float32)
     keyval = jnp.zeros((ROWS, 2 * COLS), jnp.float32)
     for j in range(TPN):
@@ -157,7 +200,6 @@
         rows = pl.ds(j * COLS, COLS)
         query += jnp.dot(normed, wq[rows, :], preferred_element_type=jnp.float32)
         keyval += jnp.dot(normed, wkv[rows, :], preferred_element_type=jnp.float32)
-    cosine, sine = cos_ref[...], sin_ref[...]
 
     def rotated(vectors):
         return (vectors * cosine + pltpu.roll(vectors, HD // 2, 1) * sine).astype(jnp.bfloat16)
@@ -182,9 +224,7 @@
     new_value = keyval[:, COLS:].astype(jnp.bfloat16)
     kv[pl.ds(0, ROWS), COLS:] = new_value
     nc_ref[:, COLS:] = new_value
-    local[3].wait()
-    for copy in p_copies:
-        copy.wait_recv()
+    forward(4)
 
     def block(i, carry):
         d, e = slot_offsets(i)
@@ -306,7 +346,7 @@
     for copies in (h_copies, q_copies, pair_copies, r_copies):
         for copy in copies.values():
             copy.wait_send()
-    for copy in p_copies + g_copies + z_copies:
+    for copy in sum(p_steps, []) + g_copies + z_copies:
         copy.wait_send()
     for i in range(1, 7):
         for copy in returned(i):
@@ -316,19 +356,11 @@
 def local(
     hidden_in, w_query, w_keyval, w_out, prompt_cache, tail_cache, tail_table, tail_len, shared_len
 ):
-    s = lax.axis_index("seq")
     half = HD // 2
-    positions = (
-        shared_len[0]
-        + lax.dynamic_index_in_dim(tail_len, s // REQ, 0, keepdims=False)
-        + (s % REQ) * ROWS
-        + jnp.arange(ROWS, dtype=jnp.int32)
-    )
-    freqs = 10000.0 ** (-jnp.arange(half, dtype=jnp.float32) / half)
-    angles = positions.astype(jnp.float32)[:, None] * freqs
-    cosine, sine = jnp.cos(angles), jnp.sin(angles)
-    cosine = jnp.concatenate([cosine, cosine], axis=1)
-    sine = jnp.concatenate([-sine, sine], axis=1)
+    freqs = 10000.0 ** (-np.arange(half, dtype=np.float64) / half)
+    table = np.zeros((8, HD), np.float32)
+    table[0] = np.concatenate([freqs, freqs])
+    table[1] = np.concatenate([-np.ones(half), np.ones(half)])
     vmem = pl.BlockSpec(memory_space=pltpu.VMEM)
     smem = pl.BlockSpec(memory_space=pltpu.SMEM)
     anywhere = pl.BlockSpec(memory_space=pl.ANY)
@@ -341,13 +373,15 @@
             jax.ShapeDtypeStruct(block, bf16),
             jax.ShapeDtypeStruct((ROWS, 2 * COLS), bf16),
         ),
-        in_specs=[smem, smem, smem, vmem, anywhere, anywhere, anywhere, vmem, anywhere, vmem, vmem],
+        in_specs=[smem, smem, smem, vmem, anywhere, anywhere, anywhere, vmem, anywhere, vmem],
         out_specs=(vmem, vmem),
         scratch_shapes=[
             pltpu.VMEM((TPN,) + block, bf16),
             pltpu.VMEM((TPN * COLS, COLS), bf16),
+            pltpu.VMEM((TPN * COLS, 2, COLS), bf16),
             pltpu.VMEM((TPN * COLS, 2 * COLS), bf16),
             pltpu.VMEM((COLS, TPN * COLS), bf16),
+            pltpu.VMEM((ROWS, 2, COLS), bf16),
             pltpu.VMEM((KEYS, 2 * COLS), bf16),
             pltpu.VMEM((8, KEYS - ROWS), f32),
             pltpu.VMEM((8,) + block, bf16),
@@ -381,12 +415,11 @@
         tail_table,
         hidden_in,
         w_query,
-        w_keyval.reshape(TPN * COLS, 2 * COLS),
+        w_keyval,
         w_out,
-        prompt_cache.reshape(128, 2 * COLS),
-        tail_cache.reshape(ROWS, 2 * COLS),
-        cosine,
-        sine,
+        prompt_cache,
+        tail_cache.reshape(ROWS, 2, COLS),
+        jnp.asarray(table),
     )
     return (out, cache.reshape(ROWS, 2, COLS))
 

time: 105 us -> 84.1 us (0.80)
  Pallas kernels: 90.6 us -> 79.3 us
  local copies, waits for them, and re-layouts: 11.2 us -> 3.28 us
  other arithmetic: 1.4 us -> 0 us
    pallas_call x1, Pallas kernels: 90.6 us -> 79.3 us  [local(): pl.pallas_call(kernel, out_shape=(jax.ShapeDtypeStruct(block, bf16), jax....]
    unnamed x4 -> x1, local copies, waits for them, and re-layouts: 8.2 us -> 1.57 us
    dynamic_slice x1 -> x0, local copies, waits for them, and re-layouts: 1.24 us -> none  [local(): lax.dynamic_index_in_dim(tail_len, s // REQ, 0, keepdims=False)]
where the time goes in v2:
time: 84.1 us; the launch traced here: 83.9 us
  Pallas kernels  79.3 us (94%)
  local copies, waits for them, and re-layouts  3.28 us (4%)
  between operations  1.29 us (2%)
    pallas_call x1, Pallas kernels, local(): pl.pallas_call(kernel, out_shape=(jax.ShapeDtypeStruct(block, bf16), jax....  79.3 us
    reshape x1, local copies, waits for them, and re-layouts, local(): return (out, cache.reshape(ROWS, 2, COLS))  1.72 us

profile of v2, /device:TPU:1, one launch (start us, length us, event | category | flops | bytes accessed | tf_op | source)
XLA Modules:
  0.0 83.9 jit_solution(11126906671482475859)
XLA Ops:
  1.3 79.3 %shard_map.113 = (bf16[256,256]{1,0:T(8,128)(2,1)}, bf16[256,512]{1,0:T(8,128)(2,1)}) custom-call(s32[1]{0:T(128)S(6)} %copy.13.shared_ref, s32[8]{0:T(128)} %tail_len_ref.1, s32[8,16]{1,0:T(8,128)} %table_ref.1, bf16[256,256]{1,0:T(8,128)(2,1)} %hid.1, bf16[2048,256]{1,0:T(8,128)(2,1)} %wq_hbm.1, bf16[2048,2,256]{2,1,0:T(2,128)(2,1)} %wkv_hbm.1, ...), custom_call_target="tpu_custom_call" | custom-call | tf_op jit(solution)/shard_map/pallas_call | solution.py:370
  80.6 1.7 %reshape.11 = bf16[256,2,256]{2,1,0:T(2,128)(2,1)} reshape(bf16[256,512]{1,0:T(8,128)(2,1)} %get-tuple-element.5) | data formatting | bytes 524288 | tf_op jit(solution)/shard_map/reshape | solution.py:424
  82.3 1.6 %copy.14 = bf16[256,256]{1,0:T(8,128)(2,1)} copy(bf16[256,256]{1,0:T(8,128)(2,1)} %get-tuple-element.8) | data formatting | bytes 262144

commit v3 on v2

v3 whole, which is shorter than its diff:
```python
import functools

import jax
import jax.numpy as jnp
import numpy as np
from jax import lax
from jax.experimental import pallas as pl
from jax.experimental.pallas import tpu as pltpu
from jax.sharding import PartitionSpec as P

HD = 128
REQ = 8
ROWS = 256
COLS = 256
TPN = 8
KEYS = 1536
NEG = -1e30
SCALE = HD**-0.5 * 1.4426950408889634
MESH = pl.DeviceIdType.MESH


def flip(v, d):
    low = (v % 2 + d % 2) % 2
    high = (v // 2 + d // 2) % 2
    return low + 2 * high


def mix(parts, stats):
    top = functools.reduce(jnp.maximum, [s[0:1] for s in stats])
    raw = [s[1:2] * jnp.exp2(s[0:1] - top) for s in stats]
    total = sum(raw)
    pad = jnp.zeros((128 - len(stats), ROWS), jnp.float32)
    columns = jnp.concatenate([w / total for w in raw] + [pad], axis=0).T
    mixed = sum(columns[:, j : j + 1] * part.astype(jnp.float32) for j, part in enumerate(parts))
    return mixed, top, total


def kernel(
    shared_ref, tail_len_ref, table_ref, hid, wq_hbm, wkv_hbm, wo_hbm, prompt, tail_hbm,
    freq_ref, out_ref, nc_ref,
    hbuf, wq, wkv_raw, wkv, wo, tail_raw, kv, bias, qbuf, obuf, sbuf, obuf_in, sbuf_in, zo, zs, zo_in, zs_in,
    nbuf, wo_in, att, att_in, rs_out, rs_in,
    lsem, p_send, p_recv, h_send, h_recv, g_send, g_recv, q_send, q_recv, o_send, o_recv,
    s_send, s_recv, w_send, w_recv, a_send, a_recv, r_send, r_recv,
):
    s = lax.axis_index("seq")
    t = lax.axis_index("tp")
    y, x, zh = s // 8, (s // 2) % 4, s % 2
    zl, c = t // 2, t % 2
    member = s % 8
    pair = (s, zl * 2 + 1 - c)
    zpeer = (y * 8 + x * 2 + 1 - zh, t)

    def tp_peer(d):
        return (s, flip(zl, d) * 2 + c)

    def x_peer(d):
        return (y * 8 + flip(x, d) * 2 + zh, t)

    def y_peer(d):
        return (((y + d) % 8) * 8 + x * 2 + zh, t)

    def remote(src, dst, send, recv, device):
        return pltpu.make_async_remote_copy(
            src_ref=src, dst_ref=dst, send_sem=send, recv_sem=recv, device_id=device,
            device_id_type=MESH,
        )

    local = [
        pltpu.make_async_copy(wq_hbm, wq, lsem.at[0]),
        pltpu.make_async_copy(wkv_hbm, wkv_raw, lsem.at[1]),
        pltpu.make_async_copy(wo_hbm, wo, lsem.at[2]),
        pltpu.make_async_copy(tail_hbm, tail_raw, lsem.at[3]),
    ]
    for copy in local:
        copy.start()

    kv[pl.ds(512, 128), 0:COLS] = prompt[:, 0, :]
    kv[pl.ds(512, 128), COLS:] = prompt[:, 1, :]

    barrier = pltpu.get_barrier_semaphore()
    peers = [pair, zpeer]
    peers += [tp_peer(d) for d in (1, 2, 3)]
    peers += [x_peer(d) for d in (1, 2, 3)]
    peers += [y_peer(1), y_peer(7)]
    for peer in peers:
        pl.semaphore_signal(barrier, inc=1, device_id=peer, device_id_type=MESH)
    pl.semaphore_wait(barrier, len(peers))

    h_copies = {}
    for d in (3, 2, 1):
        h_copies[d] = remote(hid, hbuf.at[t], h_send.at[d], h_recv.at[d], tp_peer(d))
        h_copies[d].start()
    h_copies[0] = remote(hid, hbuf.at[t], h_send.at[0], h_recv.at[0], pair)
    h_copies[0].start()
    def ring(step):
        first = 64 if step == 4 else 128
        right = remote(
            kv.at[pl.ds(512 + (step - 1) * 128, first), :],
            kv.at[pl.ds(512 + step * 128, first), :],
            p_send.at[step - 1], p_recv.at[step - 1], y_peer(1),
        )
        shift = 128 - first
        left = remote(
            kv.at[pl.ds(512 + (9 - step) % 8 * 128 + shift, first), :],
            kv.at[pl.ds(512 + (8 - step) * 128 + shift, first), :],
            p_send.at[step + 3], p_recv.at[step + 3], y_peer(7),
        )
        return [right, left]

    p_steps = [ring(step) for step in (1, 2, 3, 4)]

    def forward(step):
        if step > 0:
            for copy in p_steps[step - 1]:
                copy.wait_recv()
        if step < 4:
            for copy in p_steps[step]:
                copy.start()

    forward(0)

    hbuf[t] = hid[...]
    own_tail = tail_len_ref[y]
    shared = shared_ref[0]
    lane = lax.broadcasted_iota(jnp.int32, (8, 128), 1)
    for k in range(2):
        block = jnp.int32(0)
        for j in range(16):
            block += jnp.where(table_ref[y, j] == s * 2 + k, jnp.int32(j), jnp.int32(0))
        bias[:, k * 128 : (k + 1) * 128] = jnp.where(block * 128 + lane < own_tail, 0.0, NEG)
    for d in range(8):
        start = (((y + 8 - d) % 8) * 8 + x * 2 + zh) * 128
        bias[:, 256 + d * 128 : 384 + d * 128] = jnp.where(start + lane < shared, 0.0, NEG)

    positions = shared + own_tail + member * ROWS
    positions = positions + lax.broadcasted_iota(jnp.int32, (ROWS, HD), 0)
    angles = positions.astype(jnp.float32) * freq_ref[0:1, :]
    cosine = jnp.cos(angles)
    sine = jnp.sin(angles) * freq_ref[1:2, :]
    local[3].wait()
    kv[pl.ds(256, 256), 0:COLS] = tail_raw[:, 0, :]
    kv[pl.ds(256, 256), COLS:] = tail_raw[:, 1, :]
    local[1].wait()

    def unweave(k, carry):
        rows = pl.ds(pl.multiple_of(k * 256, 256), 256)
        wkv[rows, 0:COLS] = wkv_raw[rows, 0, :]
        wkv[rows, COLS:] = wkv_raw[rows, 1, :]
        return carry

    lax.fori_loop(0, 4, unweave, 0)
    forward(1)
    local[2].wait()
    w_copies = []
    for d in range(4):
        start = pl.multiple_of((flip(zl, d) * 2 + 1 - c) * COLS, COLS)
        w_copies.append(
            remote(wo.at[:, pl.ds(start, COLS)], wo_in.at[d], w_send.at[d], w_recv.at[d], pair)
        )
        w_copies[d].start()
    lax.fori_loop(4, 8, unweave, 0)
    forward(2)

    g_copies = []
    for d in (1, 2, 3):
        h_copies[d].wait_recv()
        index = flip(zl, d) * 2 + c
        copy = remote(hbuf.at[index], hbuf.at[index], g_send.at[d], g_recv.at[d], pair)
        copy.start()
        g_copies.append(copy)
    forward(3)
    h_copies[0].wait_recv()
    for copy in g_copies:
        copy.wait_recv()

    total = functools.reduce(
        jnp.add, [hbuf[j].astype(jnp.float32) for j in range(TPN)]
    )
    mean = jnp.sum(total, axis=1, keepdims=True) * (1.0 / (TPN * COLS))
    square = jnp.zeros((ROWS, COLS), jnp.float32)
    for j in range(TPN):
        centred = hbuf[j].astype(jnp.float32) - mean
        square += centred * centred
    spread = jnp.sum(square, axis=1, keepdims=True) * (1.0 / (TPN * COLS))
    factor = lax.rsqrt(spread + 1e-05)
    local[0].wait()
    query = jnp.zeros((ROWS, COLS), jnp.float32)
    for j in range(TPN):
        normed = ((hbuf[j].astype(jnp.float32) - mean) * factor).astype(jnp.bfloat16)
        nbuf[j] = normed
        query += jnp.dot(
            normed, wq[pl.ds(j * COLS, COLS), :], preferred_element_type=jnp.float32
        )

    def rotated(vectors):
        return (vectors * cosine + pltpu.roll(vectors, HD // 2, 1) * sine).astype(jnp.bfloat16)

    q_copies = {}
    for h in range(2):
        qbuf[h, 0] = rotated(query[:, h * HD : (h + 1) * HD])
        for slot in (4, 1, 3, 2):
            q_copies[h, slot] = remote(
                qbuf.at[h, 0], qbuf.at[h, slot], q_send.at[h, slot], q_recv.at[h, slot],
                zpeer if slot == 4 else x_peer(slot),
            )
            q_copies[h, slot].start()
        for slot in (5, 7, 6):
            q_copies[h, slot] = remote(
                qbuf.at[h, 4], qbuf.at[h, slot], q_send.at[h, slot], q_recv.at[h, slot],
                x_peer(slot - 4),
            )
    keyval = jnp.zeros((ROWS, 2 * COLS), jnp.float32)
    for j in range(TPN):
        keyval += jnp.dot(
            nbuf[j], wkv[pl.ds(j * COLS, COLS), :], preferred_element_type=jnp.float32
        )
    for h in range(2):
        lanes = slice(h * HD, (h + 1) * HD)
        new_key = rotated(keyval[:, lanes])
        kv[pl.ds(0, ROWS), lanes] = new_key
        nc_ref[:, lanes] = new_key
    new_value = keyval[:, COLS:].astype(jnp.bfloat16)
    kv[pl.ds(0, ROWS), COLS:] = new_value
    nc_ref[:, COLS:] = new_value
    forward(4)

    def returned(h, slot, d):
        return (
            remote(
                sbuf.at[h, slot], sbuf_in.at[h, slot], s_send.at[h, slot], s_recv.at[h, slot],
                x_peer(d),
            ),
            remote(
                obuf.at[h, slot], obuf_in.at[h, slot], o_send.at[h, slot], o_recv.at[h, slot],
                x_peer(d),
            ),
        )

    def attend(h, slot, d, e):
        other = flip(x, d) * 2 + (zh + e) % 2
        column = lax.broadcasted_iota(jnp.int32, (ROWS, ROWS), 1)
        row = lax.broadcasted_iota(jnp.int32, (ROWS, ROWS), 0)
        causal = column - row <= (other - member) * ROWS
        values = slice(COLS + h * HD, COLS + (h + 1) * HD)
        scores = lax.dot_general(
            qbuf[h, slot], kv[:, h * HD : (h + 1) * HD], (((1,), (1,)), ((), ())),
            preferred_element_type=jnp.float32,
        ) * SCALE
        fresh = jnp.where(causal, scores[:, :ROWS], NEG)
        cached = scores[:, ROWS:] + bias[0:1, :]
        top = jnp.maximum(
            jnp.max(fresh, axis=1, keepdims=True), jnp.max(cached, axis=1, keepdims=True)
        )
        fresh = jnp.exp2(fresh - top)
        cached = jnp.exp2(cached - top)
        total = jnp.sum(fresh, axis=1, keepdims=True) + jnp.sum(cached, axis=1, keepdims=True)
        mixed = jnp.dot(
            fresh.astype(jnp.bfloat16), kv[0:ROWS, values], preferred_element_type=jnp.float32
        ) + jnp.dot(
            cached.astype(jnp.bfloat16), kv[ROWS:KEYS, values], preferred_element_type=jnp.float32
        )
        obuf[h, slot] = (mixed / total).astype(jnp.bfloat16)
        place = lax.broadcasted_iota(jnp.int32, (ROWS, 128), 1)
        sbuf[h, slot] = jnp.where(place == 0, top, total).T[0:8]

    def arrive(h, slot, d):
        remote(
            qbuf.at[h, 0], qbuf.at[h, slot], q_send.at[h, slot], q_recv.at[h, slot], x_peer(d)
        ).wait_recv()

    def give(h, slot, d):
        for copy in returned(h, slot, d):
            copy.start()

    def near(h, first, last):
        def body(i, carry):
            d = i + i // 2 - 2 * (i // 3)

            @pl.when(i > 0)
            def _():
                arrive(h, d, d)

            attend(h, d, d, 0)

            @pl.when(i > 0)
            def _():
                give(h, d, d)

            return carry

        lax.fori_loop(first, last, body, 0)

    def far(h):
        def body(i, carry):
            d = i + i // 2 - 2 * (i // 3)
            arrive(h, 4 + d, d)
            attend(h, 4 + d, d, 1)
            give(h, 4 + d, d)
            return carry

        lax.fori_loop(1, 4, body, 0)

    def relay(h):
        q_copies[h, 4].wait_recv()
        for slot in (5, 7, 6):
            q_copies[h, slot].start()

    def joined(h, own):
        others = [own + d for d in (1, 2, 3)]
        for slot in others:
            for copy in returned(h, slot, slot - own):
                copy.wait_recv()
        return mix(
            [obuf[h, own]] + [obuf_in[h, slot] for slot in others],
            [sbuf[h, own]] + [sbuf_in[h, slot] for slot in others],
        )

    z_copies = []

    def across(h):
        mixed, top, total = joined(h, 4)
        zo[h] = mixed.astype(jnp.bfloat16)
        zs[h] = jnp.concatenate([top, total] * 4, axis=0)
        z_copies.append(remote(zs.at[h], zs_in.at[h], s_send.at[h, 4], s_recv.at[h, 4], zpeer))
        z_copies.append(remote(zo.at[h], zo_in.at[h], o_send.at[h, 4], o_recv.at[h, 4], zpeer))
        for copy in z_copies[-2:]:
            copy.start()

    near(0, 0, 4)
    near(1, 0, 2)
    relay(0)
    near(1, 2, 4)
    relay(1)
    attend(0, 4, 0, 1)
    far(0)
    attend(1, 4, 0, 1)
    across(0)
    far(1)
    across(1)
    a_copies = []
    for h in range(2):
        mixed, top, total = joined(h, 0)
        for copy in z_copies[2 * h : 2 * h + 2]:
            copy.wait_recv()
        mixed, _, _ = mix(
            [mixed, zo_in[h]], [jnp.concatenate([top, total] * 4, axis=0), zs_in[h]]
        )
        att[h] = mixed.astype(jnp.bfloat16)
        a_copies.append(remote(att.at[h], att_in.at[h], a_send.at[h], a_recv.at[h], pair))
        a_copies[h].start()

    own = jnp.concatenate([att[0], att[1]], axis=1)
    for copy in w_copies + a_copies:
        copy.wait_recv()
    partner = jnp.concatenate([att_in[0], att_in[1]], axis=1)

    def share(d):
        start = pl.multiple_of((flip(zl, d) * 2 + c) * COLS, COLS)
        return jnp.dot(
            own, wo[:, pl.ds(start, COLS)], preferred_element_type=jnp.float32
        ) + jnp.dot(partner, wo_in[d], preferred_element_type=jnp.float32)

    r_copies = {}
    for d in (3, 2, 1):
        rs_out[d] = share(d).astype(jnp.bfloat16)
        r_copies[d] = remote(rs_out.at[d], rs_in.at[d], r_send.at[d], r_recv.at[d], tp_peer(d))
        r_copies[d].start()
    summed = hid[...].astype(jnp.float32) + share(0)
    for d in (1, 2, 3):
        r_copies[d].wait_recv()
        summed += rs_in[d].astype(jnp.float32)
    out_ref[...] = summed.astype(jnp.bfloat16)

    for copies in (h_copies, q_copies, r_copies):
        for copy in copies.values():
            copy.wait_send()
    for copy in sum(p_steps, []) + g_copies + z_copies + w_copies + a_copies:
        copy.wait_send()
    for h in range(2):
        for slot in (1, 2, 3, 5, 6, 7):
            for copy in returned(h, slot, slot % 4):
                copy.wait_send()


def local(
    hidden_in, w_query, w_keyval, w_out, prompt_cache, tail_cache, tail_table, tail_len, shared_len
):
    half = HD // 2
    freqs = 10000.0 ** (-np.arange(half, dtype=np.float64) / half)
    table = np.zeros((8, HD), np.float32)
    table[0] = np.concatenate([freqs, freqs])
    table[1] = np.concatenate([-np.ones(half), np.ones(half)])
    vmem = pl.BlockSpec(memory_space=pltpu.VMEM)
    smem = pl.BlockSpec(memory_space=pltpu.SMEM)
    anywhere = pl.BlockSpec(memory_space=pl.ANY)
    bf16, f32 = jnp.bfloat16, jnp.float32
    dma = pltpu.SemaphoreType.DMA
    block = (ROWS, COLS)
    out, cache = pl.pallas_call(
        kernel,
        out_shape=(
            jax.ShapeDtypeStruct(block, bf16),
            jax.ShapeDtypeStruct((ROWS, 2 * COLS), bf16),
        ),
        in_specs=[smem, smem, smem, vmem, anywhere, anywhere, anywhere, vmem, anywhere, vmem],
        out_specs=(vmem, vmem),
        scratch_shapes=[
            pltpu.VMEM((TPN,) + block, bf16),
            pltpu.VMEM((TPN * COLS, COLS), bf16),
            pltpu.VMEM((TPN * COLS, 2, COLS), bf16),
            pltpu.VMEM((TPN * COLS, 2 * COLS), bf16),
            pltpu.VMEM((COLS, TPN * COLS), bf16),
            pltpu.VMEM((ROWS, 2, COLS), bf16),
            pltpu.VMEM((KEYS, 2 * COLS), bf16),
            pltpu.VMEM((8, KEYS - ROWS), f32),
            pltpu.VMEM((2, 8, ROWS, HD), bf16),
            pltpu.VMEM((2, 8, ROWS, HD), bf16),
            pltpu.VMEM((2, 8, 8, ROWS), f32),
            pltpu.VMEM((2, 8, ROWS, HD), bf16),
            pltpu.VMEM((2, 8, 8, ROWS), f32),
            pltpu.VMEM((2, ROWS, HD), bf16),
            pltpu.VMEM((2, 8, ROWS), f32),
            pltpu.VMEM((2, ROWS, HD), bf16),
            pltpu.VMEM((2, 8, ROWS), f32),
            pltpu.VMEM((TPN,) + block, bf16),
            pltpu.VMEM((4,) + block, bf16),
            pltpu.VMEM((2, ROWS, HD), bf16),
            pltpu.VMEM((2, ROWS, HD), bf16),
            pltpu.VMEM((4,) + block, bf16),
            pltpu.VMEM((4,) + block, bf16),
            dma((4,)),
            dma((8,)), dma((8,)),
            dma((4,)), dma((4,)),
            dma((4,)), dma((4,)),
            dma((2, 8)), dma((2, 8)),
            dma((2, 8)), dma((2, 8)),
            dma((2, 8)), dma((2, 8)),
            dma((4,)), dma((4,)),
            dma((2,)), dma((2,)),
            dma((4,)), dma((4,)),
        ],
        compiler_params=pltpu.CompilerParams(collective_id=0, has_side_effects=True),
    )(
        shared_len,
        tail_len,
        tail_table,
        hidden_in,
        w_query,
        w_keyval,
        w_out,
        prompt_cache,
        tail_cache.reshape(ROWS, 2, COLS),
        jnp.asarray(table),
    )
    return (out, cache.reshape(ROWS, 2, COLS))


def solution(mesh):
    return jax.shard_map(
        local,
        mesh=mesh,
        in_specs=(
            P("seq", "tp"),
            P(None, "tp"),
            P(None, None, "tp"),
            P("tp", None),
            P("seq", None, "tp"),
            P("seq", None, None, "tp"),
            P(),
            P(),
            P(),
        ),
        out_specs=(P("seq", "tp"), P("seq", None, "tp")),
        check_vma=False,
    )
```

time: 84.1 us -> 87.4 us (1.039)
  Pallas kernels: 79.3 us -> 82.6 us
    pallas_call x1, Pallas kernels: 79.3 us -> 82.6 us  [local(): pl.pallas_call(kernel, out_shape=(jax.ShapeDtypeStruct(block, bf16), jax....]
where the time goes in v3:
time: 87.4 us; the launch traced here: 87.2 us
  Pallas kernels  82.6 us (95%)
  local copies, waits for them, and re-layouts  3.28 us (4%)
  between operations  1.29 us (1%)
    pallas_call x1, Pallas kernels, local(): pl.pallas_call(kernel, out_shape=(jax.ShapeDtypeStruct(block, bf16), jax....  82.6 us

profile of v3, /device:TPU:1, one launch (start us, length us, event | category | flops | bytes accessed | tf_op | source)
XLA Modules:
  0.0 87.2 jit_solution(997625396937123303)
XLA Ops:
  1.3 82.6 %shard_map.113 = (bf16[256,256]{1,0:T(8,128)(2,1)}, bf16[256,512]{1,0:T(8,128)(2,1)}) custom-call(s32[1]{0:T(128)S(6)} %copy.13.shared_ref, s32[8]{0:T(128)} %tail_len_ref.1, s32[8,16]{1,0:T(8,128)} %table_ref.1, bf16[256,256]{1,0:T(8,128)(2,1)} %hid.1, bf16[2048,256]{1,0:T(8,128)(2,1)} %wq_hbm.1, bf16[2048,2,256]{2,1,0:T(2,128)(2,1)} %wkv_hbm.1, ...), custom_call_target="tpu_custom_call" | custom-call | tf_op jit(solution)/shard_map/pallas_call | solution.py:400
  83.9 1.7 %reshape.11 = bf16[256,2,256]{2,1,0:T(2,128)(2,1)} reshape(bf16[256,512]{1,0:T(8,128)(2,1)} %get-tuple-element.5) | data formatting | bytes 524288 | tf_op jit(solution)/shard_map/reshape | solution.py:456
  85.6 1.6 %copy.14 = bf16[256,256]{1,0:T(8,128)(2,1)} copy(bf16[256,256]{1,0:T(8,128)(2,1)} %get-tuple-element.8) | data formatting | bytes 262144

commit v4 on v3

--- a/solution.py
+++ b/solution.py
@@ -39,7 +39,7 @@
     shared_ref, tail_len_ref, table_ref, hid, wq_hbm, wkv_hbm, wo_hbm, prompt, tail_hbm,
     freq_ref, out_ref, nc_ref,
     hbuf, wq, wkv_raw, wkv, wo, tail_raw, kv, bias, qbuf, obuf, sbuf, obuf_in, sbuf_in, zo, zs, zo_in, zs_in,
-    nbuf, wo_in, att, att_in, rs_out, rs_in,
+    nbuf, q_hop, o_hop, v_send, v_recv, wo_in, att, att_in, rs_out, rs_in,
     lsem, p_send, p_recv, h_send, h_recv, g_send, g_recv, q_send, q_recv, o_send, o_recv,
     s_send, s_recv, w_send, w_recv, a_send, a_recv, r_send, r_recv,
 ):
@@ -60,6 +60,10 @@
     def y_peer(d):
         return (((y + d) % 8) * 8 + x * 2 + zh, t)
 
+    def z_peer(shift):
+        z = (zh * 4 + zl + shift) % 8
+        return (y * 8 + x * 2 + z // 4, z % 4 * 2 + c)
+
     def remote(src, dst, send, recv, device):
         return pltpu.make_async_remote_copy(
             src_ref=src, dst_ref=dst, send_sem=send, recv_sem=recv, device_id=device,
@@ -83,6 +87,7 @@
     peers += [tp_peer(d) for d in (1, 2, 3)]
     peers += [x_peer(d) for d in (1, 2, 3)]
     peers += [y_peer(1), y_peer(7)]
+    peers += [z_peer(shift) for shift in (1, 7, 3, 5)]
     for peer in peers:
         pl.semaphore_signal(barrier, inc=1, device_id=peer, device_id_type=MESH)
     pl.semaphore_wait(barrier, len(peers))
@@ -151,14 +156,6 @@
 
     lax.fori_loop(0, 4, unweave, 0)
     forward(1)
-    local[2].wait()
-    w_copies = []
-    for d in range(4):
-        start = pl.multiple_of((flip(zl, d) * 2 + 1 - c) * COLS, COLS)
-        w_copies.append(
-            remote(wo.at[:, pl.ds(start, COLS)], wo_in.at[d], w_send.at[d], w_recv.at[d], pair)
-        )
-        w_copies[d].start()
     lax.fori_loop(4, 8, unweave, 0)
     forward(2)
 
@@ -196,25 +193,38 @@
     def rotated(vectors):
         return (vectors * cosine + pltpu.roll(vectors, HD // 2, 1) * sine).astype(jnp.bfloat16)
 
+    q_down = remote(qbuf.at[1, 0], q_hop, v_send.at[0], v_recv.at[0], z_peer(7))
     q_copies = {}
     for h in range(2):
         qbuf[h, 0] = rotated(query[:, h * HD : (h + 1) * HD])
         for slot in (4, 1, 3, 2):
+            down = slot == 4 and h == 1
             q_copies[h, slot] = remote(
-                qbuf.at[h, 0], qbuf.at[h, slot], q_send.at[h, slot], q_recv.at[h, slot],
-                zpeer if slot == 4 else x_peer(slot),
+                q_hop if down else qbuf.at[h, 0],
+                qbuf.at[h, slot], q_send.at[h, slot], q_recv.at[h, slot],
+                x_peer(slot) if slot < 4 else z_peer(5) if down else zpeer,
             )
-            q_copies[h, slot].start()
+            (q_down if down else q_copies[h, slot]).start()
         for slot in (5, 7, 6):
             q_copies[h, slot] = remote(
                 qbuf.at[h, 4], qbuf.at[h, slot], q_send.at[h, slot], q_recv.at[h, slot],
                 x_peer(slot - 4),
             )
+    local[2].wait()
+    w_copies = []
+    for d in range(4):
+        start = pl.multiple_of((flip(zl, d) * 2 + 1 - c) * COLS, COLS)
+        w_copies.append(
+            remote(wo.at[:, pl.ds(start, COLS)], wo_in.at[d], w_send.at[d], w_recv.at[d], pair)
+        )
+        w_copies[d].start()
     keyval = jnp.zeros((ROWS, 2 * COLS), jnp.float32)
     for j in range(TPN):
         keyval += jnp.dot(
             nbuf[j], wkv[pl.ds(j * COLS, COLS), :], preferred_element_type=jnp.float32
         )
+    q_down.wait_recv()
+    q_copies[1, 4].start()
     for h in range(2):
         lanes = slice(h * HD, (h + 1) * HD)
         new_key = rotated(keyval[:, lanes])
@@ -317,27 +327,38 @@
         )
 
     z_copies = []
+    o_down = remote(zo.at[1], o_hop, v_send.at[1], v_recv.at[1], z_peer(7))
 
     def across(h):
         mixed, top, total = joined(h, 4)
         zo[h] = mixed.astype(jnp.bfloat16)
         zs[h] = jnp.concatenate([top, total] * 4, axis=0)
         z_copies.append(remote(zs.at[h], zs_in.at[h], s_send.at[h, 4], s_recv.at[h, 4], zpeer))
-        z_copies.append(remote(zo.at[h], zo_in.at[h], o_send.at[h, 4], o_recv.at[h, 4], zpeer))
-        for copy in z_copies[-2:]:
-            copy.start()
+        z_copies[-1].start()
+        if h == 0:
+            z_copies.append(
+                remote(zo.at[0], zo_in.at[0], o_send.at[0, 4], o_recv.at[0, 4], zpeer)
+            )
+            z_copies[-1].start()
+        else:
+            o_down.start()
+            z_copies.append(
+                remote(o_hop, zo_in.at[1], o_send.at[1, 4], o_recv.at[1, 4], z_peer(5))
+            )
 
     near(0, 0, 4)
     near(1, 0, 2)
     relay(0)
     near(1, 2, 4)
+    attend(0, 4, 0, 1)
     relay(1)
-    attend(0, 4, 0, 1)
     far(0)
     attend(1, 4, 0, 1)
     across(0)
     far(1)
     across(1)
+    o_down.wait_recv()
+    z_copies[3].start()
     a_copies = []
     for h in range(2):
         mixed, top, total = joined(h, 0)
@@ -375,7 +396,7 @@
     for copies in (h_copies, q_copies, r_copies):
         for copy in copies.values():
             copy.wait_send()
-    for copy in sum(p_steps, []) + g_copies + z_copies + w_copies + a_copies:
+    for copy in sum(p_steps, []) + g_copies + z_copies + w_copies + a_copies + [q_down, o_down]:
         copy.wait_send()
     for h in range(2):
         for slot in (1, 2, 3, 5, 6, 7):
@@ -424,6 +445,9 @@
             pltpu.VMEM((2, ROWS, HD), bf16),
             pltpu.VMEM((2, 8, ROWS), f32),
             pltpu.VMEM((TPN,) + block, bf16),
+            pltpu.VMEM((ROWS, HD), bf16),
+            pltpu.VMEM((ROWS, HD), bf16),
+            dma((2,)), dma((2,)),
             pltpu.VMEM((4,) + block, bf16),
             pltpu.VMEM((2, ROWS, HD), bf16),
             pltpu.VMEM((2, ROWS, HD), bf16),

time: 87.4 us -> 94.3 us (1.079); the launches traced: 87.2 us -> 93 us
  Pallas kernels: 82.6 us -> 88.4 us
    pallas_call x1, Pallas kernels: 82.6 us -> 88.4 us  [local(): pl.pallas_call(kernel, out_shape=(jax.ShapeDtypeStruct(block, bf16), jax....]
where the time goes in v4:
time: 94.3 us; the launch traced here: 93 us
  Pallas kernels  88.4 us (94%)
  local copies, waits for them, and re-layouts  3.28 us (3%)
  between operations  1.29 us (1%)
    pallas_call x1, Pallas kernels, local(): pl.pallas_call(kernel, out_shape=(jax.ShapeDtypeStruct(block, bf16), jax....  88.4 us

profile of v4, /device:TPU:1, one launch (start us, length us, event | category | flops | bytes accessed | tf_op | source)
XLA Modules:
  0.0 93.0 jit_solution(1626689335802518494)
XLA Ops:
  1.3 88.4 %shard_map.113 = (bf16[256,256]{1,0:T(8,128)(2,1)}, bf16[256,512]{1,0:T(8,128)(2,1)}) custom-call(s32[1]{0:T(128)S(6)} %copy.13.shared_ref, s32[8]{0:T(128)} %tail_len_ref.1, s32[8,16]{1,0:T(8,128)} %table_ref.1, bf16[256,256]{1,0:T(8,128)(2,1)} %hid.1, bf16[2048,256]{1,0:T(8,128)(2,1)} %wq_hbm.1, bf16[2048,2,256]{2,1,0:T(2,128)(2,1)} %wkv_hbm.1, ...), custom_call_target="tpu_custom_call" | custom-call | tf_op jit(solution)/shard_map/pallas_call | solution.py:421
  89.7 1.7 %reshape.11 = bf16[256,2,256]{2,1,0:T(2,128)(2,1)} reshape(bf16[256,512]{1,0:T(8,128)(2,1)} %get-tuple-element.5) | data formatting | bytes 524288 | tf_op jit(solution)/shard_map/reshape | solution.py:480
  91.4 1.6 %copy.14 = bf16[256,256]{1,0:T(8,128)(2,1)} copy(bf16[256,256]{1,0:T(8,128)(2,1)} %get-tuple-element.8) | data formatting | bytes 262144

commit v5 on v2

--- a/solution.py
+++ b/solution.py
@@ -55,9 +55,9 @@
     shared_ref, tail_len_ref, table_ref, hid, wq_hbm, wkv_hbm, wo_hbm, prompt, tail_hbm,
     freq_ref, out_ref, nc_ref,
     hbuf, wq, wkv_raw, wkv, wo, tail_raw, kv, bias, qbuf, obuf, sbuf, obuf_in, sbuf_in, zo, zs, zo_in, zs_in,
-    pair_out, pair_in, acc, rs_out, rs_in,
+    wo_in, att, att_in, rs_out, rs_in,
     lsem, p_send, p_recv, h_send, h_recv, g_send, g_recv, q_send, q_recv, o_send, o_recv,
-    s_send, s_recv, w_send, w_recv, r_send, r_recv,
+    s_send, s_recv, w_send, w_recv, a_send, a_recv, r_send, r_recv,
 ):
     s = lax.axis_index("seq")
     t = lax.axis_index("tp")
@@ -216,6 +216,14 @@
     for i in (4, 5, 6):
         d, _ = slot_offsets(i)
         q_copies[i] = remote(qbuf.at[7], qbuf.at[i], q_send.at[i], q_recv.at[i], x_peer(d))
+    local[2].wait()
+    w_copies = []
+    for d in range(4):
+        start = pl.multiple_of((flip(zl, d) * 2 + 1 - c) * COLS, COLS)
+        w_copies.append(
+            remote(wo.at[:, pl.ds(start, COLS)], wo_in.at[d], w_send.at[d], w_recv.at[d], pair)
+        )
+        w_copies[d].start()
     for h in range(2):
         lanes = slice(h * HD, (h + 1) * HD)
         new_key = rotated(keyval[:, lanes])
@@ -315,38 +323,34 @@
     mixed, _, _ = mix(
         [mixed, zo_in[...]], [jnp.concatenate([top, total], axis=0), zs_in[...]]
     )
-    attended = mixed.astype(jnp.bfloat16)
-
-    local[2].wait()
-
-    def share(d, core):
-        start = pl.multiple_of((flip(zl, d) * 2 + core) * COLS, COLS)
-        return jnp.dot(attended, wo[:, pl.ds(start, COLS)], preferred_element_type=jnp.float32)
-
-    pair_copies = {}
-    for d in (3, 2, 1, 0):
-        pair_out[d] = share(d, 1 - c).astype(jnp.bfloat16)
-        pair_copies[d] = remote(pair_out.at[d], pair_in.at[d], w_send.at[d], w_recv.at[d], pair)
-        pair_copies[d].start()
-    for d in (3, 2, 1, 0):
-        acc[d] = share(d, c)
+    att[...] = mixed.astype(jnp.bfloat16)
+    a_copy = remote(att, att_in, a_send.at[0], a_recv.at[0], pair)
+    a_copy.start()
+
+    for copy in w_copies + [a_copy]:
+        copy.wait_recv()
+
+    def share(d):
+        start = pl.multiple_of((flip(zl, d) * 2 + c) * COLS, COLS)
+        return jnp.dot(
+            att[...], wo[:, pl.ds(start, COLS)], preferred_element_type=jnp.float32
+        ) + jnp.dot(att_in[...], wo_in[d], preferred_element_type=jnp.float32)
+
     r_copies = {}
     for d in (3, 2, 1):
-        pair_copies[d].wait_recv()
-        rs_out[d] = (acc[d] + pair_in[d].astype(jnp.float32)).astype(jnp.bfloat16)
+        rs_out[d] = share(d).astype(jnp.bfloat16)
         r_copies[d] = remote(rs_out.at[d], rs_in.at[d], r_send.at[d], r_recv.at[d], tp_peer(d))
         r_copies[d].start()
-    pair_copies[0].wait_recv()
-    summed = hid[...].astype(jnp.float32) + acc[0] + pair_in[0].astype(jnp.float32)
+    summed = hid[...].astype(jnp.float32) + share(0)
     for d in (1, 2, 3):
         r_copies[d].wait_recv()
         summed += rs_in[d].astype(jnp.float32)
     out_ref[...] = summed.astype(jnp.bfloat16)
 
-    for copies in (h_copies, q_copies, pair_copies, r_copies):
+    for copies in (h_copies, q_copies, r_copies):
         for copy in copies.values():
             copy.wait_send()
-    for copy in sum(p_steps, []) + g_copies + z_copies:
+    for copy in sum(p_steps, []) + g_copies + z_copies + w_copies + [a_copy]:
         copy.wait_send()
     for i in range(1, 7):
         for copy in returned(i):
@@ -394,8 +398,8 @@
             pltpu.VMEM(block, bf16),
             pltpu.VMEM((8, ROWS), f32),
             pltpu.VMEM((4,) + block, bf16),
-            pltpu.VMEM((4,) + block, bf16),
-            pltpu.VMEM((4,) + block, f32),
+            pltpu.VMEM(block, bf16),
+            pltpu.VMEM(block, bf16),
             pltpu.VMEM((4,) + block, bf16),
             pltpu.VMEM((4,) + block, bf16),
             dma((4,)),
@@ -406,6 +410,7 @@
             dma((8,)), dma((8,)),
             dma((8,)), dma((8,)),
             dma((4,)), dma((4,)),
+            dma((1,)), dma((1,)),
             dma((4,)), dma((4,)),
         ],
         compiler_params=pltpu.CompilerParams(collective_id=0, has_side_effects=True),

time: 84.1 us -> 84.4 us (level)
  no operation moved by 1% of the time
where the time goes in v5:
time: 84.4 us; the launch traced here: 84.2 us
  Pallas kernels  79.7 us (94%)
  local copies, waits for them, and re-layouts  3.28 us (4%)
  between operations  1.29 us (2%)
    pallas_call x1, Pallas kernels, local(): pl.pallas_call(kernel, out_shape=(jax.ShapeDtypeStruct(block, bf16), jax....  79.7 us
    reshape x1, local copies, waits for them, and re-layouts, local(): return (out, cache.reshape(ROWS, 2, COLS))  1.72 us

profile of v5, /device:TPU:1, one launch (start us, length us, event | category | flops | bytes accessed | tf_op | source)
XLA Modules:
  0.0 84.2 jit_solution(9143897391838717676)
XLA Ops:
  1.3 79.7 %shard_map.113 = (bf16[256,256]{1,0:T(8,128)(2,1)}, bf16[256,512]{1,0:T(8,128)(2,1)}) custom-call(s32[1]{0:T(128)S(6)} %copy.13.shared_ref, s32[8]{0:T(128)} %tail_len_ref.1, s32[8,16]{1,0:T(8,128)} %table_ref.1, bf16[256,256]{1,0:T(8,128)(2,1)} %hid.1, bf16[2048,256]{1,0:T(8,128)(2,1)} %wq_hbm.1, bf16[2048,2,256]{2,1,0:T(2,128)(2,1)} %wkv_hbm.1, ...), custom_call_target="tpu_custom_call" | custom-call | tf_op jit(solution)/shard_map/pallas_call | solution.py:374
  80.9 1.7 %reshape.11 = bf16[256,2,256]{2,1,0:T(2,128)(2,1)} reshape(bf16[256,512]{1,0:T(8,128)(2,1)} %get-tuple-element.5) | data formatting | bytes 524288 | tf_op jit(solution)/shard_map/reshape | solution.py:429
  82.7 1.6 %copy.14 = bf16[256,256]{1,0:T(8,128)(2,1)} copy(bf16[256,256]{1,0:T(8,128)(2,1)} %get-tuple-element.8) | data formatting | bytes 262144
